TPU v7x, 512 devices: a whole 4x4x16 slice. The times are simulated.
512 devices in a mesh: sa: 32 (over z, core), sb: 16 (over x, y).
Axes of the slice: x: 4, y: 4, z: 16, core: 2. Of those that a mesh axis runs over, the one named last changes fastest.
Arguments:
- queries: bfloat16 [65536, 16, 192], P(('sa', 'sb')), may hold values from -110 to 110
- keys: bfloat16 [65536, 192], P(('sa', 'sb')), may hold values from -6 to 6
- values: bfloat16 [65536, 128], P(('sa', 'sb')), may hold values from -6 to 6
- key_first: bfloat16 [6144, 192], replicated, may hold values from -0.078125 to 0.078125
- key_second: bfloat16 [192, 192], replicated, may hold values from -0.4375 to 0.4375
- value_first: bfloat16 [4096, 128], replicated, may hold values from -0.09375 to 0.09375
- value_second: bfloat16 [128, 128], replicated, may hold values from -0.5 to 0.5
- gate_table: float32 [16, 2], replicated, may hold values from 0.1 to 1
- gate_index: int32 [65536, 16], P(('sa', 'sb')), may hold values from 0 to 15
Outputs:
- mixed: bfloat16 [65536, 16, 128], P(('sa', 'sb'))
All inputs are finite; a program needn't handle non-finite values.
Results may differ from a plain program's by a relative error of at most 0.0053.
Values may be sent and summed in bfloat16 or wider, within the bound.
No kernel may reach another device: no remote copies, remote signals or barrier semaphores. Data moves between devices by JAX's collectives and lax.ppermute only.
A program may use at most 64 MiB of HBM per device.

v0:
```python
import functools

import jax
import jax.numpy as jnp
from jax import lax
from jax.experimental import pallas as pl
from jax.experimental.pallas import tpu as pltpu
from jax.sharding import PartitionSpec as P


STRIDE = 16
LOG2E = 1.4426950408889634
LOW = -1e30
FLOOR = -1e29
GRANT = 20 << 20


def nt(a, b):
    return lax.dot_general(a, b, (((1,), (1,)), ((), ())), preferred_element_type=jnp.float32)


def shifted(shard, axis, by):
    size = lax.axis_size(axis)
    pairs = [(i, i + by) for i in range(size) if 0 <= i + by < size]
    return lax.ppermute(shard, axis, pairs)


def pair_kernel(keys_ref, values_ref, out_ref):
    out_ref[:, :192] = keys_ref[...].astype(jnp.float32).T.astype(out_ref.dtype)
    out_ref[:, 192:256] = jnp.zeros((out_ref.shape[0], 64), out_ref.dtype)
    out_ref[:, 256:] = values_ref[...]


def pair(keys, values):
    return pl.pallas_call(
        pair_kernel,
        in_specs=[pl.BlockSpec(memory_space=pltpu.VMEM)] * 2,
        out_specs=pl.BlockSpec(memory_space=pltpu.VMEM),
        out_shape=jax.ShapeDtypeStruct((keys.shape[0], 384), keys.dtype),
        compiler_params=pltpu.CompilerParams(vmem_limit_bytes=GRANT),
        name="pair",
    )(keys.T, values)


def silu(x):
    return x * (1.0 / (1.0 + jnp.exp(-x)))


def segments(wide_ref, count):
    keys, values = [], []
    for first in range(STRIDE):
        some = [wide_ref[part, pl.ds(first, count, stride=STRIDE), :] for part in range(3)]
        keys.append(jnp.concatenate([some[0], some[1][:, :64]], axis=1))
        values.append(some[2])
    keys = jnp.concatenate(keys, axis=1).astype(jnp.bfloat16)
    values = jnp.concatenate(values, axis=1).astype(jnp.bfloat16)
    return keys, values


def own_kernel(pair_ref, kfirst_ref, vfirst_ref, hidden_ref, wide):
    half_keys = kfirst_ref.shape[1] // 2
    half_values = vfirst_ref.shape[0] // 2
    count = pair_ref.shape[0] // STRIDE
    for part in range(3):
        lanes = slice(128 * part, 128 * part + 128)
        wide[part] = pair_ref[:, lanes].astype(jnp.float32)
    keys, values = segments(wide, count)
    nothing = jnp.zeros((count, 64), jnp.float32)
    back = jnp.concatenate(
        [
            nt(keys, kfirst_ref[:, half_keys:]),
            nothing,
            jnp.dot(values, vfirst_ref[half_values:], preferred_element_type=jnp.float32),
        ],
        axis=1,
    )
    ahead = jnp.concatenate(
        [
            nt(keys, kfirst_ref[:, :half_keys]),
            nothing,
            jnp.dot(values, vfirst_ref[:half_values], preferred_element_type=jnp.float32),
        ],
        axis=1,
    )
    row = lax.broadcasted_iota(jnp.int32, back.shape, 0)
    hidden_ref[...] = back + jnp.where(row == 0, 0.0, pltpu.roll(ahead, 1, 0))


def own_blocks(paired, kfirst, vfirst):
    rows = paired.shape[0]
    inside = pl.BlockSpec(memory_space=pltpu.VMEM)
    return pl.pallas_call(
        own_kernel,
        in_specs=[inside] * 3,
        out_specs=inside,
        out_shape=jax.ShapeDtypeStruct((rows // STRIDE, 384), jnp.float32),
        scratch_shapes=[pltpu.VMEM((3, rows, 128), jnp.float32)],
        compiler_params=pltpu.CompilerParams(vmem_limit_bytes=GRANT),
        name="own_blocks",
        cost_estimate=pl.CostEstimate(
            flops=1000000000, bytes_accessed=8000000, transcendentals=0
        ),
    )(paired, kfirst, vfirst)


def summary_kernel(
    before_ref, hidden_ref, kfirst_ref, ksecond_ref, vfirst_ref, vsecond_ref, out_ref, wide
):
    rows = before_ref.shape[0]
    count = hidden_ref.shape[0]
    for part in range(3):
        lanes = slice(128 * part, 128 * part + 128)
        wide[part] = before_ref[:, lanes].astype(jnp.float32)
    keys, values = segments(wide, rows // STRIDE)
    ahead = jnp.concatenate(
        [
            nt(keys, kfirst_ref[:, : kfirst_ref.shape[1] // 2]),
            jnp.zeros((count, 64), jnp.float32),
            jnp.dot(
                values,
                vfirst_ref[: vfirst_ref.shape[0] // 2],
                preferred_element_type=jnp.float32,
            ),
        ],
        axis=1,
    )
    row = lax.broadcasted_iota(jnp.int32, ahead.shape, 0)
    hidden = hidden_ref[...] + jnp.where(row == 0, pltpu.roll(ahead, 1, 0), 0.0)
    hidden = silu(hidden).astype(jnp.bfloat16)
    key = jnp.dot(hidden[:, :192], ksecond_ref[...], preferred_element_type=jnp.float32)
    value = jnp.dot(hidden[:, 256:], vsecond_ref[...], preferred_element_type=jnp.float32)
    high = jnp.concatenate([key[:, 128:], jnp.zeros((count, 64), jnp.float32)], axis=1)
    payload = jnp.concatenate([key[:, :128], high, value], axis=0).astype(out_ref.dtype)
    for copy in range(out_ref.shape[0]):
        out_ref[copy] = payload


def summary(before, hidden, kfirst, key_second, vfirst, value_second, copies):
    inside = pl.BlockSpec(memory_space=pltpu.VMEM)
    default = pl.BlockSpec()
    return pl.pallas_call(
        summary_kernel,
        in_specs=[inside, inside, inside, default, inside, default],
        out_specs=inside,
        out_shape=jax.ShapeDtypeStruct((copies, 3 * hidden.shape[0], 128), jnp.bfloat16),
        scratch_shapes=[pltpu.VMEM((3,) + (before.shape[0], 128), jnp.float32)],
        compiler_params=pltpu.CompilerParams(vmem_limit_bytes=GRANT),
        name="summary",
    )(before, hidden, kfirst, key_second, vfirst, value_second)


def pack_kernel(column_ref, out_ref):
    planes = column_ref.shape[0]
    half = planes // 2
    count = column_ref.shape[1] // 3
    low = column_ref[:, :count].astype(jnp.float32).reshape(planes * count, 128)
    high = column_ref[:, count : 2 * count].astype(jnp.float32)
    high = jnp.concatenate(
        [
            high[:half].reshape(half * count, 128)[:, :64],
            high[half:].reshape(half * count, 128)[:, :64],
        ],
        axis=1,
    )
    value = column_ref[:, 2 * count :].astype(jnp.float32).reshape(planes * count, 128)
    packed = jnp.concatenate([low, high, value], axis=0).astype(out_ref.dtype)
    for copy in range(out_ref.shape[0]):
        out_ref[copy] = packed


def pack(column, copies):
    planes, rows, lanes = column.shape
    inside = pl.BlockSpec(memory_space=pltpu.VMEM)
    return pl.pallas_call(
        pack_kernel,
        in_specs=[inside],
        out_specs=inside,
        out_shape=jax.ShapeDtypeStruct((copies, planes * rows * 5 // 6, lanes), column.dtype),
        compiler_params=pltpu.CompilerParams(vmem_limit_bytes=GRANT),
        name="pack",
    )(column)


def window_kernel(
    scale, heads, who, q_ref, four_ref, two_ref, one_ref, pair_ref, gate_ref, out_ref, *scratch
):
    sub = scratch[0].shape[0]
    size = pair_ref.shape[0]
    blocks = q_ref.shape[0] // sub
    device = who[0]
    base = pl.program_id(0) * (q_ref.shape[0] // heads)
    near = (
        jnp.concatenate([four_ref[...], two_ref[:size]], axis=0),
        jnp.concatenate([two_ref[size:], one_ref[...]], axis=0),
        pair_ref[...],
    )
    begins = [
        size * jnp.clip(4 - device, 0, 2),
        size * jnp.clip(2 - device, 0, 2),
    ]

    def score(j):
        s_ref = scratch[j % 2]
        q = q_ref[j * sub : (j + 1) * sub]
        q = jnp.concatenate([q, jnp.zeros((sub, 64), q.dtype)], axis=1)
        token = base + j * (sub // heads) + lax.broadcasted_iota(jnp.int32, (sub, 256), 0) // heads
        lane = lax.broadcasted_iota(jnp.int32, (sub, 256), 1)
        s0 = nt(q, near[0][:, :256])
        s0 = jnp.where(lane > jnp.maximum(token, begins[0] - 1), s0, LOW)
        s1 = nt(q, near[1][:, :256])
        s1 = jnp.where(lane >= begins[1], s1, LOW)
        s2 = nt(q, near[2][:, :256])
        s2 = jnp.where(lane[:, :128] <= token[:, :128], s2, LOW)
        s_ref[:, :256] = s0
        s_ref[:, 256:512] = s1
        s_ref[:, 512:] = s2
        top = jnp.maximum(jnp.maximum(s0, s1), jnp.concatenate([s2, s2], axis=1))
        return jnp.maximum(jnp.max(top, axis=1, keepdims=True), FLOOR)

    def mix(j, top):
        s_ref = scratch[j % 2]
        accum = jnp.zeros((sub, 256), jnp.float32)
        for part, at in enumerate((0, 256, 512)):
            wide = near[part].shape[0]
            p = jnp.exp2((s_ref[:, at : at + wide] - top) * (scale * LOG2E)).astype(jnp.bfloat16)
            v = jnp.concatenate([near[part][:, 256:], jnp.ones((wide, 128), jnp.bfloat16)], axis=1)
            accum += jnp.dot(p, v, preferred_element_type=jnp.float32)
        here = slice(j * sub, (j + 1) * sub)
        out_ref[here] = gate_ref[here, 1:2] * (accum[:, :128] / accum[:, 128:])

    tops = [score(0)]
    for j in range(blocks):
        if j + 1 < blocks:
            tops.append(score(j + 1))
        mix(j, tops[j])


def window_branch(who, q, four, two, one, paired, gates, scale, heads, block=1024, sub=256):
    total = q.shape[0]

    def row(width):
        return pl.BlockSpec((block, width), lambda i, w: (i, 0))

    def whole(array):
        return pl.BlockSpec(array.shape, lambda i, w: (0, 0))

    return pl.pallas_call(
        functools.partial(window_kernel, scale, heads),
        grid_spec=pltpu.PrefetchScalarGridSpec(
            num_scalar_prefetch=1,
            grid=(total // block,),
            in_specs=[
                row(q.shape[1]),
                whole(four),
                whole(two),
                whole(one),
                whole(paired),
                row(2),
            ],
            out_specs=row(128),
            scratch_shapes=[pltpu.VMEM((sub, 640), jnp.float32)] * 2,
        ),
        out_shape=jax.ShapeDtypeStruct((total, 128), jnp.float32),
        compiler_params=pltpu.CompilerParams(vmem_limit_bytes=GRANT),
        name="window",
        cost_estimate=pl.CostEstimate(
            flops=2 * total * 640 * 512, bytes_accessed=4000000, transcendentals=total * 640
        ),
    )(who, q, four, two, one, paired, gates)


def far_scores(heads, device, core, q, kv_ref, s_ref, base, quarters):
    block = q.shape[0]
    zeros = jnp.zeros((block, 64), q.dtype)
    queries = (
        jnp.concatenate([q, zeros], axis=1),
        jnp.concatenate([q[:, :128], zeros, q[:, 128:]], axis=1),
    )
    token = base + lax.broadcasted_iota(jnp.int32, (block, 256), 0) // heads
    lane = lax.broadcasted_iota(jnp.int32, (1, 256), 1)
    top = None
    for quarter in range(quarters):
        for g in range(kv_ref.shape[0] // 8):
            some = slice(8 * g, 8 * g + 8)
            begin = 32 * quarter
            low = kv_ref[some, begin : begin + 32].reshape(256, 128)
            begin = 128 + 32 * (quarter % 2)
            high = kv_ref[some, begin : begin + 32].reshape(256, 128)
            s = nt(queries[quarter // 2], jnp.concatenate([low, high], axis=1))
            z = 4 * quarter + (lane % 32) // 8
            owner = (2 * z + core) * 16 + 8 * g + lane // 32
            end = (owner - device) * 128 + STRIDE * (lane % 8) + STRIDE - 1
            s = jnp.where(end <= token, s, LOW)
            slot = 2 * quarter + g
            s_ref[:, 256 * slot : 256 * slot + 256] = s
            most = jnp.maximum(s[:, :128], s[:, 128:])
            top = most if top is None else jnp.maximum(top, most)
    return jnp.maximum(jnp.max(top, axis=1, keepdims=True), FLOOR)


def far_mix(scale, s_ref, top, kv_ref, quarters):
    ones = jnp.ones((256, 128), jnp.bfloat16)
    accum = jnp.zeros((s_ref.shape[0], 256), jnp.float32)
    for quarter in range(quarters):
        for g in range(kv_ref.shape[0] // 8):
            slot = 2 * quarter + g
            s = s_ref[:, 256 * slot : 256 * slot + 256]
            p = jnp.exp2((s - top) * (scale * LOG2E)).astype(jnp.bfloat16)
            begin = 192 + 32 * quarter
            v = kv_ref[8 * g : 8 * g + 8, begin : begin + 32].reshape(256, 128)
            accum += jnp.dot(
                p, jnp.concatenate([v, ones], axis=1), preferred_element_type=jnp.float32
            )
    return accum


def skewed(scale, heads, who, core, q_ref, kv_ref, scratch, finish):
    sub = scratch[0].shape[0]
    blocks = q_ref.shape[0] // sub
    base = pl.program_id(0) * (q_ref.shape[0] // heads)
    plane = who[2]

    def run(quarters):
        def score(j):
            return far_scores(
                heads,
                who[0],
                core,
                q_ref[j * sub : (j + 1) * sub],
                kv_ref,
                scratch[j % 2],
                base + j * (sub // heads),
                quarters,
            )

        tops = [score(0)]
        for j in range(blocks):
            if j + 1 < blocks:
                tops.append(score(j + 1))
            mix = far_mix(scale, scratch[j % 2], tops[j], kv_ref, quarters)
            finish(slice(j * sub, (j + 1) * sub), mix, tops[j])

    @pl.when(plane < 4)
    def _():
        run(1)

    @pl.when((plane >= 4) & (plane < 8))
    def _():
        run(2)

    @pl.when(plane >= 8)
    def _():
        run(4)


def first_kernel(scale, heads, who, q_ref, kv_ref, acc_ref, top_ref, *scratch):
    def finish(here, accum, top):
        acc_ref[here] = accum
        top_ref[here] = jnp.broadcast_to(top, (accum.shape[0], 128))

    skewed(scale, heads, who, who[1], q_ref, kv_ref, scratch, finish)


def second_kernel(
    scale, heads, who, q_ref, kv_ref, acc_ref, top_ref, win_ref, gate_ref, out_ref, *scratch
):
    def finish(here, accum, top):
        other = top_ref[here]
        most = jnp.maximum(other, top)
        grow = jnp.exp2((other - most) * (scale * LOG2E))
        shrink = jnp.exp2((top - most) * (scale * LOG2E))
        number = acc_ref[here, :128] * grow + accum[:, :128] * shrink
        total = acc_ref[here, 128:] * grow + accum[:, 128:] * shrink
        present = total > 0.0
        compressed = jnp.where(present, number / jnp.where(present, total, 1.0), 0.0)
        out_ref[here] = (gate_ref[here, 0:1] * compressed + win_ref[here]).astype(out_ref.dtype)

    skewed(scale, heads, who, 1 - who[1], q_ref, kv_ref, scratch, finish)


def first_half(who, q, kv, scale, heads, block=2048, sub=256):
    total = q.shape[0]
    keys = kv.shape[0] * 128
    return pl.pallas_call(
        functools.partial(first_kernel, scale, heads),
        grid_spec=pltpu.PrefetchScalarGridSpec(
            num_scalar_prefetch=1,
            grid=(total // block,),
            in_specs=[
                pl.BlockSpec((block, q.shape[1]), lambda i, w: (i, 0)),
                pl.BlockSpec(memory_space=pltpu.VMEM),
            ],
            out_specs=[
                pl.BlockSpec((block, 256), lambda i, w: (i, 0)),
                pl.BlockSpec((block, 128), lambda i, w: (i, 0)),
            ],
            scratch_shapes=[pltpu.VMEM((sub, keys), jnp.float32)] * 2,
        ),
        out_shape=[
            jax.ShapeDtypeStruct((total, 256), jnp.float32),
            jax.ShapeDtypeStruct((total, 128), jnp.float32),
        ],
        compiler_params=pltpu.CompilerParams(vmem_limit_bytes=GRANT),
        name="first_half",
        cost_estimate=pl.CostEstimate(
            flops=2 * total * keys * 512, bytes_accessed=3000000, transcendentals=total * keys
        ),
    )(who, q, kv)


def second_half(who, q, kv, acc, top, win, gates, scale, heads, block=2048, sub=256):
    total = q.shape[0]
    keys = kv.shape[0] * 128

    def row(width):
        return pl.BlockSpec((block, width), lambda i, w: (i, 0))

    return pl.pallas_call(
        functools.partial(second_kernel, scale, heads),
        grid_spec=pltpu.PrefetchScalarGridSpec(
            num_scalar_prefetch=1,
            grid=(total // block,),
            in_specs=[
                row(q.shape[1]),
                pl.BlockSpec(memory_space=pltpu.VMEM),
                row(256),
                row(128),
                row(128),
                row(2),
            ],
            out_specs=row(128),
            scratch_shapes=[pltpu.VMEM((sub, keys), jnp.float32)] * 2,
        ),
        out_shape=jax.ShapeDtypeStruct((total, 128), jnp.bfloat16),
        compiler_params=pltpu.CompilerParams(vmem_limit_bytes=GRANT),
        name="second_half",
        cost_estimate=pl.CostEstimate(
            flops=2 * total * keys * 512, bytes_accessed=5000000, transcendentals=total * keys
        ),
    )(who, q, kv, acc, top, win, gates)


def local(
    queries, keys, values, key_first, key_second, value_first, value_second, gate_table, gate_index
):
    rows, heads, depth = queries.shape
    outer, inner = lax.axis_index("sa"), lax.axis_index("sb")
    core = outer % 2
    device = outer * lax.axis_size("sb") + inner
    who = jnp.stack([device, core, outer // 2]).astype(jnp.int32)
    planes = lax.axis_size("sa") // 2
    scale = depth ** (-0.5)
    paired = pair(keys, values)
    one = shifted(paired, ("sa", "sb"), 1)
    kfirst = key_first.T
    hidden = own_blocks(paired, kfirst, value_first)
    payload = summary(one, hidden, kfirst, key_second, value_first, value_second, planes)
    payload, later, again = lax.optimization_barrier((payload, one, paired))
    groups = [[2 * z + c for z in range(planes)] for c in range(2)]
    column = lax.all_to_all(payload, "sa", 0, 0, axis_index_groups=groups)
    four = shifted(again, ("sa", "sb"), 4)
    two = shifted(jnp.concatenate([later, again], axis=0), ("sa", "sb"), 2)
    query_rows = queries.reshape(rows * heads, depth)
    chosen = gate_index.reshape(rows * heads)
    onehot = (chosen[:, None] == lax.iota(jnp.int32, gate_table.shape[0])[None, :]).astype(
        jnp.float32
    )
    gates = jnp.sum(onehot[:, :, None] * gate_table[None, :, :], axis=1)
    copies = pack(column, lax.axis_size("sb"))
    mine = lax.all_to_all(copies, "sb", 0, 0)
    win = window_branch(who, query_rows, four, two, later, again, gates, scale, heads)
    mine, win = lax.optimization_barrier((mine, win))
    other = lax.ppermute(mine, "sa", [(i, i ^ 1) for i in range(2 * planes)])
    acc, top = first_half(who, query_rows, mine, scale, heads)
    mixed = second_half(who, query_rows, other, acc, top, win, gates, scale, heads)
    return mixed.reshape(rows, heads, values.shape[1])


def solution(mesh):
    in_specs = (
        P(("sa", "sb"), None, None),
        P(("sa", "sb"), None),
        P(("sa", "sb"), None),
        P(),
        P(),
        P(),
        P(),
        P(),
        P(("sa", "sb"), None),
    )
    out_specs = P(("sa", "sb"), None, None)
    return jax.shard_map(local, mesh=mesh, in_specs=in_specs, out_specs=out_specs, check_vma=False)
```

profile of v0, /device:TPU:481, one launch (start us, length us, event | category | flops | bytes accessed | tf_op | source)
XLA Modules:
  0.0 84.4 jit_solution(11108036477614838041)
XLA Ops:
  0.0 0.0 copy-start.7
  0.0 0.8 copy-done.7
  0.8 0.8 copy-done.9
  1.6 0.1 pair.1.pair_ref
  1.7 3.2 %collective-permute-start = (bf16[128,384]{1,0:T(8,128)(2,1)S(1)}, bf16[128,384]{1,0:T(8,128)(2,1)S(1)}, u32[]{:S(2)}, u32[]{:S(2)}) collective-permute-start(bf16[128,384]{1,0:T(8,128)(2,1)S(1)} %pair.1.pair_ref), channel_id=1, source_target_pairs={{0,1},{1,2},{2,3},{3,4},{4,5},{5,6},{6,7},{7,8},{8,9},{9,10},{10,1... | collective-permute-start | bytes 294920 | tf_op jit(solution)/shard_map/ppermute | solution.py:25
  4.9 0.0 copy-start
  4.9 1.7 %copy-done = bf16[6144,192]{0,1:T(8,128)(2,1)S(1)} copy-done((bf16[6144,192]{0,1:T(8,128)(2,1)S(1)}, bf16[6144,192]{0,1:T(8,128)(2,1)}, u32[]{:S(2)}) %copy-start) | copy-done | bytes 2359320
  6.5 0.0 copy-start.2
  6.5 1.2 %copy-done.2 = bf16[4096,128]{1,0:T(8,128)(2,1)S(1)} copy-done((bf16[4096,128]{1,0:T(8,128)(2,1)S(1)}, bf16[4096,128]{1,0:T(8,128)(2,1)}, u32[]{:S(2)}) %copy-start.2) | copy-done | bytes 1048600
  7.8 0.0 copy-start.1
  7.8 0.0 copy-start.3
  7.8 0.0 copy-start.6
  7.8 0.0 copy-start.8
  7.8 0.9 %own_blocks.1.hidden_ref = f32[8,384]{1,0:T(8,128)S(1)} custom-call(bf16[128,384]{1,0:T(8,128)(2,1)S(1)} %pair.1.pair_ref, bf16[192,6144]{1,0:T(8,128)(2,1)S(1)} %bitcast.7, bf16[4096,128]{1,0:T(8,128)(2,1)S(1)} %copy-done.2), custom_call_target="tpu_custom_call" | custom-call | flops 1000000000 | bytes 8000000 | tf_op jit(solution)/shard_map/own_blocks/pallas_call | solution.py:92
  8.7 3.7 %collective-permute-done.before_ref.one_ref = bf16[128,384]{1,0:T(8,128)(2,1)S(1)} collective-permute-done((bf16[128,384]{1,0:T(8,128)(2,1)S(1)}, bf16[128,384]{1,0:T(8,128)(2,1)S(1)}, u32[]{:S(2)}, u32[]{:S(2)}) %collective-permute-start) | collective-permute-done | bytes 98336 | tf_op jit(solution)/shard_map/ppermute | solution.py:25
  12.4 0.0 copy-done.1
  12.4 0.0 copy-done.3
  12.4 0.0 copy-done.6
  12.4 0.0 copy-done.8
  12.4 0.0 copy-start.4
  12.4 0.7 summary.1
  13.1 18.9 %all_to_all.10.column_ref = bf16[16,24,128]{2,1,0:T(8,128)(2,1)S(1)} all-to-all(bf16[16,24,128]{2,1,0:T(8,128)(2,1)S(1)} %summary.1), channel_id=1, replica_groups={{0,32,64,96,128,160,192,224,256,288,320,352,384,416,448,480},{16,48,80,..., dimensions={0} | all-to-all | bytes 196608 | tf_op jit(solution)/shard_map/all_to_all | solution.py:460
  32.1 1.2 %pack.1 = bf16[16,320,128]{2,1,0:T(8,128)(2,1)} custom-call(bf16[16,24,128]{2,1,0:T(8,128)(2,1)S(1)} %all_to_all.10.column_ref), custom_call_target="tpu_custom_call" | custom-call | tf_op jit(solution)/shard_map/pack/pallas_call | solution.py:174
  33.3 4.5 %all-to-all-start.1 = ((bf16[16,320,128]{2,1,0:T(8,128)(2,1)}), bf16[16,320,128]{2,1,0:T(8,128)(2,1)S(1)}, u32[]{:S(2)}, u32[]{:S(2)}) async-start(bf16[16,320,128]{2,1,0:T(8,128)(2,1)} %pack.1), calls=%async_computation.1 | async-start | bytes 2621440 | tf_op jit(solution)/shard_map/all_to_all | solution.py:470
  37.8 0.0 copy-done.12
  37.8 0.1 copy.16
  37.9 0.1 eq.21
  38.0 0.0 copy-done.4
  38.1 0.7 pad_maximum_fusion
  38.8 4.7 %collective-permute-start.2 = (bf16[256,384]{1,0:T(8,128)(2,1)}, bf16[256,384]{1,0:T(8,128)(2,1)}, u32[]{:S(2)}, u32[]{:S(2)}) collective-permute-start(bf16[256,384]{1,0:T(8,128)(2,1)} %pad_maximum_fusion), channel_id=1, source_target_pairs={{0,2},{1,3},{2,4},{3,5},{4,6},{5,7},{6,8},{7,9},{8,10},{9,11},{10,... | collective-permute-start | bytes 589832 | tf_op jit(solution)/shard_map/ppermute | solution.py:25
  43.5 0.0 copy-done.13
  43.5 0.1 multiply_reduce_fusion
  43.6 0.4 copy.17.gate_ref
  44.0 1.8 %copy.15 = bf16[128,16,192]{2,1,0:T(8,128)(2,1)S(1)} copy(bf16[128,16,192]{0,2,1:T(8,128)(2,1)} %param.9) | data formatting | bytes 1572864 | tf_op args[0]
  45.9 3.1 %collective-permute-start.1 = (bf16[128,384]{1,0:T(8,128)(2,1)S(1)}, bf16[128,384]{1,0:T(8,128)(2,1)S(1)}, u32[]{:S(2)}, u32[]{:S(2)}) collective-permute-start(bf16[128,384]{1,0:T(8,128)(2,1)S(1)} %pair.1.pair_ref), channel_id=1, source_target_pairs={{0,4},{1,5},{2,6},{3,7},{4,8},{5,9},{6,10},{7,11},{8,12},{9,13},{1... | collective-permute-start | bytes 294920 | tf_op jit(solution)/shard_map/ppermute | solution.py:25
  49.0 0.1 pad_add_fusion.who
  49.0 9.3 %collective-permute-done.1.four_ref = bf16[128,384]{1,0:T(8,128)(2,1)S(1)} collective-permute-done((bf16[128,384]{1,0:T(8,128)(2,1)S(1)}, bf16[128,384]{1,0:T(8,128)(2,1)S(1)}, u32[]{:S(2)}, u32[]{:S(2)}) %collective-permute-start.1) | collective-permute-done | bytes 98336 | tf_op jit(solution)/shard_map/ppermute | solution.py:25
  58.3 5.0 %collective-permute-done.2.two_ref = bf16[256,384]{1,0:T(8,128)(2,1)} collective-permute-done((bf16[256,384]{1,0:T(8,128)(2,1)}, bf16[256,384]{1,0:T(8,128)(2,1)}, u32[]{:S(2)}, u32[]{:S(2)}) %collective-permute-start.2) | collective-permute-done | bytes 196640 | tf_op jit(solution)/shard_map/ppermute | solution.py:25
  63.4 0.9 %copy-done.5 = bf16[128,384]{1,0:T(8,128)(2,1)S(1)} copy-done((bf16[128,384]{1,0:T(8,128)(2,1)S(1)}, bf16[128,384]{1,0:T(8,128)(2,1)}, u32[]{:S(2)}) %copy-start.5) | copy-done | bytes 98328
  64.3 4.3 %window.1.win_ref = f32[2048,128]{1,0:T(8,128)S(1)} custom-call(s32[3]{0:T(128)S(1)} %pad_add_fusion.who, bf16[2048,192]{1,0:T(8,128)(2,1)S(1)} %bitcast.9, bf16[128,384]{1,0:T(8,128)(2,1)S(1)} %collective-permute-done.1.four_ref, bf16[256,384]{1,0:T(8,128)(2,1)} %collective-permute-done.2.two_ref, bf16[128,384]{1,0:T(8,128)(2,1)S(1)} %copy-done.5, ...), custom_call_target="tpu_custom_call" | custom-call | flops 1342177280 | bytes 4000000 | tf_op jit(solution)/shard_map/window/pallas_call | solution.py:247
  68.6 0.0 copy-start.10
  68.6 1.0 %copy-done.10 = f32[2048,128]{1,0:T(8,128)} copy-done((f32[2048,128]{1,0:T(8,128)}, f32[2048,128]{1,0:T(8,128)S(1)}, u32[]{:S(2)}) %copy-start.10) | copy-done | bytes 1048600
  69.5 0.0 all-to-all-done.1.kv_ref
  69.5 2.0 %collective-permute-start.3 = (bf16[16,320,128]{2,1,0:T(8,128)(2,1)S(1)}, bf16[16,320,128]{2,1,0:T(8,128)(2,1)S(1)}, u32[]{:S(2)}, u32[]{:S(2)}) collective-permute-start(bf16[16,320,128]{2,1,0:T(8,128)(2,1)S(1)} %all-to-all-done.1.kv_ref), channel_id=1, source_target_pairs={{0,16},{16,0},{32,48},{48,32},{64,80},{80,64},{96,112},{112,96},{1... | collective-permute-start | bytes 3932168 | tf_op jit(solution)/shard_map/ppermute | solution.py:473
  71.6 5.7 %first_half.1 = (f32[2048,256]{1,0:T(8,128)S(1)}, f32[2048,128]{1,0:T(8,128)S(1)}) custom-call(s32[3]{0:T(128)S(1)} %pad_add_fusion.who, bf16[2048,192]{1,0:T(8,128)(2,1)S(1)} %bitcast.10, bf16[16,320,128]{2,1,0:T(8,128)(2,1)S(1)} %all-to-all-done.1.kv_ref), custom_call_target="tpu_custom_call" | custom-call | flops 4294967296 | bytes 3000000 | tf_op jit(solution)/shard_map/first_half/pallas_call | solution.py:384
  77.3 0.0 collective-permute-done.3.kv_ref
  77.3 0.0 copy-done.11
  77.3 7.1 %second_half.1 = bf16[2048,128]{1,0:T(8,128)(2,1)} custom-call(s32[3]{0:T(128)S(1)} %pad_add_fusion.who, bf16[2048,192]{1,0:T(8,128)(2,1)S(1)} %bitcast.11, bf16[16,320,128]{2,1,0:T(8,128)(2,1)S(1)} %collective-permute-done.3.kv_ref, f32[2048,256]{1,0:T(8,128)S(1)} %get-tuple-element.16.acc_ref, f32[2048,128]{1,0:T(8,128)S(1)} %get-tuple-element.17.top_ref, ...), custom_call_target="tpu_custom_call" | custom-call | flops 4294967296 | bytes 5000000 | tf_op jit(solution)/shard_map/second_half/pallas_call | solution.py:418
  (6 shorter events, 0.0 us)
Async XLA Ops:
  0.0 0.8 copy-start.7
  0.8 0.8 copy-start.9
  1.7 10.7 %collective-permute-start = (bf16[128,384]{1,0:T(8,128)(2,1)S(1)}, bf16[128,384]{1,0:T(8,128)(2,1)S(1)}, u32[]{:S(2)}, u32[]{:S(2)}) collective-permute-start(bf16[128,384]{1,0:T(8,128)(2,1)S(1)} %pair.1.pair_ref), channel_id=1, source_target_pairs={{0,1},{1,2},{2,3},{3,4},{4,5},{5,6},{6,7},{7,8},{8,9},{9,10},{10,1... | collective-permute-start | bytes 294920 | tf_op jit(solution)/shard_map/ppermute | solution.py:25
  4.9 1.7 %copy-start = (bf16[6144,192]{0,1:T(8,128)(2,1)S(1)}, bf16[6144,192]{0,1:T(8,128)(2,1)}, u32[]{:S(2)}) copy-start(bf16[6144,192]{0,1:T(8,128)(2,1)} %param.12) | copy-start | bytes 7077892
  6.5 1.2 %copy-start.2 = (bf16[4096,128]{1,0:T(8,128)(2,1)S(1)}, bf16[4096,128]{1,0:T(8,128)(2,1)}, u32[]{:S(2)}) copy-start(bf16[4096,128]{1,0:T(8,128)(2,1)} %vfirst_ref.3) | copy-start | bytes 3145732
  7.8 4.6 %copy-start.1 = (bf16[6144,192]{0,1:T(8,128)(2,1)S(1)}, bf16[6144,192]{0,1:T(8,128)(2,1)}, u32[]{:S(2)}) copy-start(bf16[6144,192]{0,1:T(8,128)(2,1)} %param.12) | copy-start | bytes 7077892
  7.8 4.6 %copy-start.3 = (bf16[4096,128]{1,0:T(8,128)(2,1)S(1)}, bf16[4096,128]{1,0:T(8,128)(2,1)}, u32[]{:S(2)}) copy-start(bf16[4096,128]{1,0:T(8,128)(2,1)} %vfirst_ref.3) | copy-start | bytes 3145732
  7.8 4.6 %copy-start.6 = (bf16[192,192]{1,0:T(8,128)(2,1)S(1)}, bf16[192,192]{1,0:T(8,128)(2,1)}, u32[]{:S(2)}) copy-start(bf16[192,192]{1,0:T(8,128)(2,1)} %ksecond_ref.1) | copy-start | bytes 221188
  7.8 4.6 %copy-start.8 = (bf16[128,128]{1,0:T(8,128)(2,1)S(1)}, bf16[128,128]{1,0:T(8,128)(2,1)}, u32[]{:S(2)}) copy-start(bf16[128,128]{1,0:T(8,128)(2,1)} %vsecond_ref.1) | copy-start | bytes 98308
  12.4 25.6 %copy-start.4 = (bf16[128,384]{1,0:T(8,128)(2,1)}, bf16[128,384]{1,0:T(8,128)(2,1)S(1)}, u32[]{:S(2)}) copy-start(bf16[128,384]{1,0:T(8,128)(2,1)S(1)} %collective-permute-done.before_ref.one_ref) | copy-start | bytes 294916
  33.3 4.5 %copy-start.12 = (s32[128,16]{0,1:T(8,128)S(1)}, s32[128,16]{0,1:T(8,128)}, u32[]{:S(2)}) copy-start(s32[128,16]{0,1:T(8,128)} %param.17) | copy-start | bytes 24580
  33.3 10.2 %copy-start.13 = (f32[16,2]{0,1:T(2,128)S(1)}, f32[16,2]{0,1:T(2,128)}, u32[]{:S(2)}) copy-start(f32[16,2]{0,1:T(2,128)} %param.16) | copy-start | bytes 388
  33.3 36.2 %all-to-all-start.1 = ((bf16[16,320,128]{2,1,0:T(8,128)(2,1)}), bf16[16,320,128]{2,1,0:T(8,128)(2,1)S(1)}, u32[]{:S(2)}, u32[]{:S(2)}) async-start(bf16[16,320,128]{2,1,0:T(8,128)(2,1)} %pack.1), calls=%async_computation.1 | async-start | bytes 2621440 | tf_op jit(solution)/shard_map/all_to_all | solution.py:470
  38.8 24.6 %collective-permute-start.2 = (bf16[256,384]{1,0:T(8,128)(2,1)}, bf16[256,384]{1,0:T(8,128)(2,1)}, u32[]{:S(2)}, u32[]{:S(2)}) collective-permute-start(bf16[256,384]{1,0:T(8,128)(2,1)} %pad_maximum_fusion), channel_id=1, source_target_pairs={{0,2},{1,3},{2,4},{3,5},{4,6},{5,7},{6,8},{7,9},{8,10},{9,11},{10,... | collective-permute-start | bytes 589832 | tf_op jit(solution)/shard_map/ppermute | solution.py:25
  45.9 12.5 %collective-permute-start.1 = (bf16[128,384]{1,0:T(8,128)(2,1)S(1)}, bf16[128,384]{1,0:T(8,128)(2,1)S(1)}, u32[]{:S(2)}, u32[]{:S(2)}) collective-permute-start(bf16[128,384]{1,0:T(8,128)(2,1)S(1)} %pair.1.pair_ref), channel_id=1, source_target_pairs={{0,4},{1,5},{2,6},{3,7},{4,8},{5,9},{6,10},{7,11},{8,12},{9,13},{1... | collective-permute-start | bytes 294920 | tf_op jit(solution)/shard_map/ppermute | solution.py:25
  63.4 0.9 %copy-start.5 = (bf16[128,384]{1,0:T(8,128)(2,1)S(1)}, bf16[128,384]{1,0:T(8,128)(2,1)}, u32[]{:S(2)}) copy-start(bf16[128,384]{1,0:T(8,128)(2,1)} %copy-done.4) | copy-start | bytes 294916
  68.6 1.0 %copy-start.10 = (f32[2048,128]{1,0:T(8,128)}, f32[2048,128]{1,0:T(8,128)S(1)}, u32[]{:S(2)}) copy-start(f32[2048,128]{1,0:T(8,128)S(1)} %window.1.win_ref) | copy-start | bytes 3145732
  69.5 7.8 %copy-start.11 = (f32[2048,128]{1,0:T(8,128)S(1)}, f32[2048,128]{1,0:T(8,128)}, u32[]{:S(2)}) copy-start(f32[2048,128]{1,0:T(8,128)} %copy-done.10) | copy-start | bytes 3145732
  69.5 7.7 %collective-permute-start.3 = (bf16[16,320,128]{2,1,0:T(8,128)(2,1)S(1)}, bf16[16,320,128]{2,1,0:T(8,128)(2,1)S(1)}, u32[]{:S(2)}, u32[]{:S(2)}) collective-permute-start(bf16[16,320,128]{2,1,0:T(8,128)(2,1)S(1)} %all-to-all-done.1.kv_ref), channel_id=1, source_target_pairs={{0,16},{16,0},{32,48},{48,32},{64,80},{80,64},{96,112},{112,96},{1... | collective-permute-start | bytes 3932168 | tf_op jit(solution)/shard_map/ppermute | solution.py:473
where the time goes:
time: 86.1 us; the launch traced here: 84.4 us
  Pallas kernels  20 us (23%)
  blocking collectives  18.9 us (22%)
  waiting for transfers between devices  18.1 us (21%)
  starting transfers between devices  17.6 us (20%)
  local copies, waits for them, and re-layouts  8.68 us (10%)
  other arithmetic  0.92 us (1%)
    all_to_all x1, blocking collectives, local(): column = lax.all_to_all(payload, 'sa', 0, 0, axis_index_groups=groups)  18.9 us
    ppermute x3, waiting for transfers between devices, shifted(): return lax.ppermute(shard, axis, pairs)  18.1 us
    ppermute x3, starting transfers between devices, shifted(): return lax.ppermute(shard, axis, pairs)  11 us
    unnamed x30, local copies, waits for them, and re-layouts  8.24 us
    pallas_call x1, Pallas kernels, second_half(): pl.pallas_call(functools.partial(second_kernel, scale, heads), grid_spec=...  7.06 us
    pallas_call x1, Pallas kernels, first_half(): pl.pallas_call(functools.partial(first_kernel, scale, heads), grid_spec=p...  5.68 us
    all_to_all x1, starting transfers between devices, local(): mine = lax.all_to_all(copies, 'sb', 0, 0)  4.49 us
    pallas_call x1, Pallas kernels, window_branch(): pl.pallas_call(functools.partial(window_kernel, scale, heads), grid_spec=...  4.31 us
  transfers between devices with their start and end apart: 5, of which 3 were waited for; matrix products, arithmetic and copies ran while one was open for 4% of the time, Pallas kernels for 13%

commit v1 on v0

--- a/solution.py
+++ b/solution.py
@@ -149,7 +149,7 @@
     )(before, hidden, kfirst, key_second, vfirst, value_second)
 
 
-def pack_kernel(column_ref, out_ref):
+def pack_kernel(column_ref, out_hbm, packed, sems):
     planes = column_ref.shape[0]
     half = planes // 2
     count = column_ref.shape[1] // 3
@@ -163,19 +163,29 @@
         axis=1,
     )
     value = column_ref[:, 2 * count :].astype(jnp.float32).reshape(planes * count, 128)
-    packed = jnp.concatenate([low, high, value], axis=0).astype(out_ref.dtype)
-    for copy in range(out_ref.shape[0]):
-        out_ref[copy] = packed
+    packed[...] = jnp.concatenate([low, high, value], axis=0).astype(packed.dtype)
+    moves = [
+        pltpu.make_async_copy(packed, out_hbm.at[copy], sems.at[copy])
+        for copy in range(out_hbm.shape[0])
+    ]
+    for move in moves:
+        move.start()
+    for move in moves:
+        move.wait()
 
 
 def pack(column, copies):
     planes, rows, lanes = column.shape
-    inside = pl.BlockSpec(memory_space=pltpu.VMEM)
+    size = planes * rows * 5 // 6
     return pl.pallas_call(
         pack_kernel,
-        in_specs=[inside],
-        out_specs=inside,
-        out_shape=jax.ShapeDtypeStruct((copies, planes * rows * 5 // 6, lanes), column.dtype),
+        in_specs=[pl.BlockSpec(memory_space=pltpu.VMEM)],
+        out_specs=pl.BlockSpec(memory_space=pl.ANY),
+        out_shape=jax.ShapeDtypeStruct((copies, size, lanes), column.dtype),
+        scratch_shapes=[
+            pltpu.VMEM((size, lanes), column.dtype),
+            pltpu.SemaphoreType.DMA((copies,)),
+        ],
         compiler_params=pltpu.CompilerParams(vmem_limit_bytes=GRANT),
         name="pack",
     )(column)
@@ -317,7 +327,6 @@
 def skewed(scale, heads, who, core, q_ref, kv_ref, scratch, finish):
     sub = scratch[0].shape[0]
     blocks = q_ref.shape[0] // sub
-    base = pl.program_id(0) * (q_ref.shape[0] // heads)
     plane = who[2]
 
     def run(quarters):
@@ -329,7 +338,7 @@
                 q_ref[j * sub : (j + 1) * sub],
                 kv_ref,
                 scratch[j % 2],
-                base + j * (sub // heads),
+                j * (sub // heads),
                 quarters,
             )
 
@@ -362,8 +371,27 @@
 
 
 def second_kernel(
-    scale, heads, who, q_ref, kv_ref, acc_ref, top_ref, win_ref, gate_ref, out_ref, *scratch
+    scale,
+    heads,
+    who,
+    q_ref,
+    kv_ref,
+    acc_ref,
+    top_ref,
+    win_ref,
+    gate_ref,
+    out_hbm,
+    even,
+    odd,
+    result,
+    sems,
 ):
+    sub = even.shape[0]
+
+    def move(j):
+        here = slice(j * sub, (j + 1) * sub)
+        return pltpu.make_async_copy(result.at[here], out_hbm.at[here], sems.at[j])
+
     def finish(here, accum, top):
         other = top_ref[here]
         most = jnp.maximum(other, top)
@@ -373,29 +401,23 @@
         total = acc_ref[here, 128:] * grow + accum[:, 128:] * shrink
         present = total > 0.0
         compressed = jnp.where(present, number / jnp.where(present, total, 1.0), 0.0)
-        out_ref[here] = (gate_ref[here, 0:1] * compressed + win_ref[here]).astype(out_ref.dtype)
-
-    skewed(scale, heads, who, 1 - who[1], q_ref, kv_ref, scratch, finish)
-
-
-def first_half(who, q, kv, scale, heads, block=2048, sub=256):
+        result[here] = (gate_ref[here, 0:1] * compressed + win_ref[here]).astype(result.dtype)
+        move(here.start // sub).start()
+
+    skewed(scale, heads, who, 1 - who[1], q_ref, kv_ref, (even, odd), finish)
+    for j in range(q_ref.shape[0] // sub):
+        move(j).wait()
+
+
+def first_half(who, q, kv, scale, heads, sub=256):
     total = q.shape[0]
     keys = kv.shape[0] * 128
+    inside = pl.BlockSpec(memory_space=pltpu.VMEM)
     return pl.pallas_call(
         functools.partial(first_kernel, scale, heads),
-        grid_spec=pltpu.PrefetchScalarGridSpec(
-            num_scalar_prefetch=1,
-            grid=(total // block,),
-            in_specs=[
-                pl.BlockSpec((block, q.shape[1]), lambda i, w: (i, 0)),
-                pl.BlockSpec(memory_space=pltpu.VMEM),
-            ],
-            out_specs=[
-                pl.BlockSpec((block, 256), lambda i, w: (i, 0)),
-                pl.BlockSpec((block, 128), lambda i, w: (i, 0)),
-            ],
-            scratch_shapes=[pltpu.VMEM((sub, keys), jnp.float32)] * 2,
-        ),
+        in_specs=[pl.BlockSpec(memory_space=pltpu.SMEM), inside, inside],
+        out_specs=[inside, inside],
+        scratch_shapes=[pltpu.VMEM((sub, keys), jnp.float32)] * 2,
         out_shape=[
             jax.ShapeDtypeStruct((total, 256), jnp.float32),
             jax.ShapeDtypeStruct((total, 128), jnp.float32),
@@ -408,29 +430,20 @@
     )(who, q, kv)
 
 
-def second_half(who, q, kv, acc, top, win, gates, scale, heads, block=2048, sub=256):
+def second_half(who, q, kv, acc, top, win, gates, scale, heads, sub=256):
     total = q.shape[0]
     keys = kv.shape[0] * 128
-
-    def row(width):
-        return pl.BlockSpec((block, width), lambda i, w: (i, 0))
-
+    inside = pl.BlockSpec(memory_space=pltpu.VMEM)
     return pl.pallas_call(
         functools.partial(second_kernel, scale, heads),
-        grid_spec=pltpu.PrefetchScalarGridSpec(
-            num_scalar_prefetch=1,
-            grid=(total // block,),
-            in_specs=[
-                row(q.shape[1]),
-                pl.BlockSpec(memory_space=pltpu.VMEM),
-                row(256),
-                row(128),
-                row(128),
-                row(2),
-            ],
-            out_specs=row(128),
-            scratch_shapes=[pltpu.VMEM((sub, keys), jnp.float32)] * 2,
-        ),
+        in_specs=[pl.BlockSpec(memory_space=pltpu.SMEM)] + [inside] * 6,
+        out_specs=pl.BlockSpec(memory_space=pl.ANY),
+        scratch_shapes=[
+            pltpu.VMEM((sub, keys), jnp.float32),
+            pltpu.VMEM((sub, keys), jnp.float32),
+            pltpu.VMEM((total, 128), jnp.bfloat16),
+            pltpu.SemaphoreType.DMA((total // sub,)),
+        ],
         out_shape=jax.ShapeDtypeStruct((total, 128), jnp.bfloat16),
         compiler_params=pltpu.CompilerParams(vmem_limit_bytes=GRANT),
         name="second_half",

time: 86.1 us -> 85.9 us (level)
  no operation moved by 1% of the time
where the time goes in v1:
time: 85.9 us; the launch traced here: 84.4 us
  Pallas kernels  20 us (23%)
  blocking collectives  18.9 us (22%)
  waiting for transfers between devices  18.1 us (21%)
  starting transfers between devices  17.5 us (20%)
  local copies, waits for them, and re-layouts  8.69 us (10%)
  other arithmetic  0.92 us (1%)
    all_to_all x1, blocking collectives, local(): column = lax.all_to_all(payload, 'sa', 0, 0, axis_index_groups=groups)  18.9 us
    ppermute x3, waiting for transfers between devices, shifted(): return lax.ppermute(shard, axis, pairs)  18.1 us
    ppermute x3, starting transfers between devices, shifted(): return lax.ppermute(shard, axis, pairs)  11 us
    unnamed x30, local copies, waits for them, and re-layouts  8.24 us
    pallas_call x1, Pallas kernels, second_half(): pl.pallas_call(functools.partial(second_kernel, scale, heads), in_specs=[...  6.98 us
    pallas_call x1, Pallas kernels, first_half(): pl.pallas_call(functools.partial(first_kernel, scale, heads), in_specs=[p...  5.69 us
    all_to_all x1, starting transfers between devices, local(): mine = lax.all_to_all(copies, 'sb', 0, 0)  4.37 us
    pallas_call x1, Pallas kernels, window_branch(): pl.pallas_call(functools.partial(window_kernel, scale, heads), grid_spec=...  4.3 us
  transfers between devices with their start and end apart: 5, of which 3 were waited for; matrix products, arithmetic and copies ran while one was open for 4% of the time, Pallas kernels for 13%

profile of v1, /device:TPU:481, one launch (start us, length us, event | category | flops | bytes accessed | tf_op | source)
XLA Modules:
  0.0 84.4 jit_solution(7617340531451410271)
XLA Ops:
  0.0 0.0 copy-start.7
  0.0 0.8 copy-done.7
  0.8 0.8 copy-done.9
  1.6 0.1 pair.1.pair_ref
  1.7 3.2 %collective-permute-start = (bf16[128,384]{1,0:T(8,128)(2,1)S(1)}, bf16[128,384]{1,0:T(8,128)(2,1)S(1)}, u32[]{:S(2)}, u32[]{:S(2)}) collective-permute-start(bf16[128,384]{1,0:T(8,128)(2,1)S(1)} %pair.1.pair_ref), channel_id=1, source_target_pairs={{0,1},{1,2},{2,3},{3,4},{4,5},{5,6},{6,7},{7,8},{8,9},{9,10},{10,1... | collective-permute-start | bytes 294920 | tf_op jit(solution)/shard_map/ppermute | solution.py:25
  4.9 0.0 copy-start
  4.9 1.7 %copy-done = bf16[6144,192]{0,1:T(8,128)(2,1)S(1)} copy-done((bf16[6144,192]{0,1:T(8,128)(2,1)S(1)}, bf16[6144,192]{0,1:T(8,128)(2,1)}, u32[]{:S(2)}) %copy-start) | copy-done | bytes 2359320
  6.5 0.0 copy-start.2
  6.5 1.2 %copy-done.2 = bf16[4096,128]{1,0:T(8,128)(2,1)S(1)} copy-done((bf16[4096,128]{1,0:T(8,128)(2,1)S(1)}, bf16[4096,128]{1,0:T(8,128)(2,1)}, u32[]{:S(2)}) %copy-start.2) | copy-done | bytes 1048600
  7.8 0.0 copy-start.1
  7.8 0.0 copy-start.3
  7.8 0.9 %own_blocks.1.hidden_ref = f32[8,384]{1,0:T(8,128)S(1)} custom-call(bf16[128,384]{1,0:T(8,128)(2,1)S(1)} %pair.1.pair_ref, bf16[192,6144]{1,0:T(8,128)(2,1)S(1)} %bitcast.7, bf16[4096,128]{1,0:T(8,128)(2,1)S(1)} %copy-done.2), custom_call_target="tpu_custom_call" | custom-call | flops 1000000000 | bytes 8000000 | tf_op jit(solution)/shard_map/own_blocks/pallas_call | solution.py:92
  8.7 3.7 %collective-permute-done.before_ref.one_ref = bf16[128,384]{1,0:T(8,128)(2,1)S(1)} collective-permute-done((bf16[128,384]{1,0:T(8,128)(2,1)S(1)}, bf16[128,384]{1,0:T(8,128)(2,1)S(1)}, u32[]{:S(2)}, u32[]{:S(2)}) %collective-permute-start) | collective-permute-done | bytes 98336 | tf_op jit(solution)/shard_map/ppermute | solution.py:25
  12.4 0.0 copy-done.1
  12.4 0.0 copy-done.3
  12.4 0.0 copy-done.6
  12.4 0.0 copy-done.8
  12.4 0.0 copy-start.4
  12.4 0.7 summary.1
  13.1 18.9 %all_to_all.10.column_ref = bf16[16,24,128]{2,1,0:T(8,128)(2,1)S(1)} all-to-all(bf16[16,24,128]{2,1,0:T(8,128)(2,1)S(1)} %summary.1), channel_id=1, replica_groups={{0,32,64,96,128,160,192,224,256,288,320,352,384,416,448,480},{16,48,80,..., dimensions={0} | all-to-all | bytes 196608 | tf_op jit(solution)/shard_map/all_to_all | solution.py:473
  32.1 1.3 %pack.1 = bf16[16,320,128]{2,1,0:T(8,128)(2,1)} custom-call(bf16[16,24,128]{2,1,0:T(8,128)(2,1)S(1)} %all_to_all.10.column_ref), custom_call_target="tpu_custom_call" | custom-call | tf_op jit(solution)/shard_map/pack/pallas_call | solution.py:180
  33.4 0.0 copy-start.12
  33.4 0.0 copy-start.13
  33.4 4.4 %all-to-all-start.1 = ((bf16[16,320,128]{2,1,0:T(8,128)(2,1)}), bf16[16,320,128]{2,1,0:T(8,128)(2,1)S(1)}, u32[]{:S(2)}, u32[]{:S(2)}) async-start(bf16[16,320,128]{2,1,0:T(8,128)(2,1)} %pack.1), calls=%async_computation.1 | async-start | bytes 2621440 | tf_op jit(solution)/shard_map/all_to_all | solution.py:483
  37.8 0.0 copy-done.12
  37.8 0.1 copy.16
  37.9 0.1 eq.21
  38.0 0.0 copy-done.4
  38.0 0.7 pad_maximum_fusion
  38.7 4.7 %collective-permute-start.2 = (bf16[256,384]{1,0:T(8,128)(2,1)}, bf16[256,384]{1,0:T(8,128)(2,1)}, u32[]{:S(2)}, u32[]{:S(2)}) collective-permute-start(bf16[256,384]{1,0:T(8,128)(2,1)} %pad_maximum_fusion), channel_id=1, source_target_pairs={{0,2},{1,3},{2,4},{3,5},{4,6},{5,7},{6,8},{7,9},{8,10},{9,11},{10,... | collective-permute-start | bytes 589832 | tf_op jit(solution)/shard_map/ppermute | solution.py:25
  43.5 0.0 copy-done.13
  43.5 0.1 multiply_reduce_fusion
  43.6 0.4 copy.17.gate_ref
  44.0 1.8 %copy.15 = bf16[128,16,192]{2,1,0:T(8,128)(2,1)S(1)} copy(bf16[128,16,192]{0,2,1:T(8,128)(2,1)} %param.9) | data formatting | bytes 1572864 | tf_op args[0]
  45.8 3.1 %collective-permute-start.1 = (bf16[128,384]{1,0:T(8,128)(2,1)S(1)}, bf16[128,384]{1,0:T(8,128)(2,1)S(1)}, u32[]{:S(2)}, u32[]{:S(2)}) collective-permute-start(bf16[128,384]{1,0:T(8,128)(2,1)S(1)} %pair.1.pair_ref), channel_id=1, source_target_pairs={{0,4},{1,5},{2,6},{3,7},{4,8},{5,9},{6,10},{7,11},{8,12},{9,13},{1... | collective-permute-start | bytes 294920 | tf_op jit(solution)/shard_map/ppermute | solution.py:25
  48.9 0.1 pad_add_fusion.who
  49.0 9.3 %collective-permute-done.1.four_ref = bf16[128,384]{1,0:T(8,128)(2,1)S(1)} collective-permute-done((bf16[128,384]{1,0:T(8,128)(2,1)S(1)}, bf16[128,384]{1,0:T(8,128)(2,1)S(1)}, u32[]{:S(2)}, u32[]{:S(2)}) %collective-permute-start.1) | collective-permute-done | bytes 98336 | tf_op jit(solution)/shard_map/ppermute | solution.py:25
  58.3 5.0 %collective-permute-done.2.two_ref = bf16[256,384]{1,0:T(8,128)(2,1)} collective-permute-done((bf16[256,384]{1,0:T(8,128)(2,1)}, bf16[256,384]{1,0:T(8,128)(2,1)}, u32[]{:S(2)}, u32[]{:S(2)}) %collective-permute-start.2) | collective-permute-done | bytes 196640 | tf_op jit(solution)/shard_map/ppermute | solution.py:25
  63.3 0.9 %copy-done.5 = bf16[128,384]{1,0:T(8,128)(2,1)S(1)} copy-done((bf16[128,384]{1,0:T(8,128)(2,1)S(1)}, bf16[128,384]{1,0:T(8,128)(2,1)}, u32[]{:S(2)}) %copy-start.5) | copy-done | bytes 98328
  64.2 4.3 %window.1.win_ref = f32[2048,128]{1,0:T(8,128)S(1)} custom-call(s32[3]{0:T(128)S(1)} %pad_add_fusion.who, bf16[2048,192]{1,0:T(8,128)(2,1)S(1)} %bitcast.9, bf16[128,384]{1,0:T(8,128)(2,1)S(1)} %collective-permute-done.1.four_ref, bf16[256,384]{1,0:T(8,128)(2,1)} %collective-permute-done.2.two_ref, bf16[128,384]{1,0:T(8,128)(2,1)S(1)} %copy-done.5, ...), custom_call_target="tpu_custom_call" | custom-call | flops 1342177280 | bytes 4000000 | tf_op jit(solution)/shard_map/window/pallas_call | solution.py:257
  68.5 0.0 copy-start.10
  68.5 1.0 %copy-done.10 = f32[2048,128]{1,0:T(8,128)} copy-done((f32[2048,128]{1,0:T(8,128)}, f32[2048,128]{1,0:T(8,128)S(1)}, u32[]{:S(2)}) %copy-start.10) | copy-done | bytes 1048600
  69.5 0.0 all-to-all-done.1.kv_ref
  69.5 2.0 %collective-permute-start.3 = (bf16[16,320,128]{2,1,0:T(8,128)(2,1)S(1)}, bf16[16,320,128]{2,1,0:T(8,128)(2,1)S(1)}, u32[]{:S(2)}, u32[]{:S(2)}) collective-permute-start(bf16[16,320,128]{2,1,0:T(8,128)(2,1)S(1)} %all-to-all-done.1.kv_ref), channel_id=1, source_target_pairs={{0,16},{16,0},{32,48},{48,32},{64,80},{80,64},{96,112},{112,96},{1... | collective-permute-start | bytes 3932168 | tf_op jit(solution)/shard_map/ppermute | solution.py:486
  71.6 5.7 %first_half.1 = (f32[2048,256]{1,0:T(8,128)S(1)}, f32[2048,128]{1,0:T(8,128)S(1)}) custom-call(s32[3]{0:T(128)S(1)} %pad_add_fusion.who, bf16[2048,192]{1,0:T(8,128)(2,1)S(1)} %bitcast.10, bf16[16,320,128]{2,1,0:T(8,128)(2,1)S(1)} %all-to-all-done.1.kv_ref), custom_call_target="tpu_custom_call" | custom-call | flops 4294967296 | bytes 3000000 | tf_op jit(solution)/shard_map/first_half/pallas_call | solution.py:416
  77.3 0.0 collective-permute-done.3.kv_ref
  77.3 0.0 copy-done.11
  77.3 7.0 %second_half.1 = bf16[2048,128]{1,0:T(8,128)(2,1)} custom-call(s32[3]{0:T(128)S(1)} %pad_add_fusion.who, bf16[2048,192]{1,0:T(8,128)(2,1)S(1)} %bitcast.11, bf16[16,320,128]{2,1,0:T(8,128)(2,1)S(1)} %collective-permute-done.3.kv_ref, f32[2048,256]{1,0:T(8,128)S(1)} %get-tuple-element.16.acc_ref, f32[2048,128]{1,0:T(8,128)S(1)} %get-tuple-element.17.top_ref, ...), custom_call_target="tpu_custom_call" | custom-call | flops 4294967296 | bytes 5000000 | tf_op jit(solution)/shard_map/second_half/pallas_call | solution.py:437
  (6 shorter events, 0.0 us)
Async XLA Ops:
  0.0 0.8 copy-start.7
  0.8 0.8 copy-start.9
  1.7 10.7 %collective-permute-start = (bf16[128,384]{1,0:T(8,128)(2,1)S(1)}, bf16[128,384]{1,0:T(8,128)(2,1)S(1)}, u32[]{:S(2)}, u32[]{:S(2)}) collective-permute-start(bf16[128,384]{1,0:T(8,128)(2,1)S(1)} %pair.1.pair_ref), channel_id=1, source_target_pairs={{0,1},{1,2},{2,3},{3,4},{4,5},{5,6},{6,7},{7,8},{8,9},{9,10},{10,1... | collective-permute-start | bytes 294920 | tf_op jit(solution)/shard_map/ppermute | solution.py:25
  4.9 1.7 %copy-start = (bf16[6144,192]{0,1:T(8,128)(2,1)S(1)}, bf16[6144,192]{0,1:T(8,128)(2,1)}, u32[]{:S(2)}) copy-start(bf16[6144,192]{0,1:T(8,128)(2,1)} %param.12) | copy-start | bytes 7077892
  6.5 1.2 %copy-start.2 = (bf16[4096,128]{1,0:T(8,128)(2,1)S(1)}, bf16[4096,128]{1,0:T(8,128)(2,1)}, u32[]{:S(2)}) copy-start(bf16[4096,128]{1,0:T(8,128)(2,1)} %vfirst_ref.3) | copy-start | bytes 3145732
  7.8 4.6 %copy-start.1 = (bf16[6144,192]{0,1:T(8,128)(2,1)S(1)}, bf16[6144,192]{0,1:T(8,128)(2,1)}, u32[]{:S(2)}) copy-start(bf16[6144,192]{0,1:T(8,128)(2,1)} %param.12) | copy-start | bytes 7077892
  7.8 4.6 %copy-start.3 = (bf16[4096,128]{1,0:T(8,128)(2,1)S(1)}, bf16[4096,128]{1,0:T(8,128)(2,1)}, u32[]{:S(2)}) copy-start(bf16[4096,128]{1,0:T(8,128)(2,1)} %vfirst_ref.3) | copy-start | bytes 3145732
  7.8 4.6 %copy-start.6 = (bf16[192,192]{1,0:T(8,128)(2,1)S(1)}, bf16[192,192]{1,0:T(8,128)(2,1)}, u32[]{:S(2)}) copy-start(bf16[192,192]{1,0:T(8,128)(2,1)} %ksecond_ref.1) | copy-start | bytes 221188
  7.8 4.6 %copy-start.8 = (bf16[128,128]{1,0:T(8,128)(2,1)S(1)}, bf16[128,128]{1,0:T(8,128)(2,1)}, u32[]{:S(2)}) copy-start(bf16[128,128]{1,0:T(8,128)(2,1)} %vsecond_ref.1) | copy-start | bytes 98308
  12.4 25.6 %copy-start.4 = (bf16[128,384]{1,0:T(8,128)(2,1)}, bf16[128,384]{1,0:T(8,128)(2,1)S(1)}, u32[]{:S(2)}) copy-start(bf16[128,384]{1,0:T(8,128)(2,1)S(1)} %collective-permute-done.before_ref.one_ref) | copy-start | bytes 294916
  33.4 4.4 %copy-start.12 = (s32[128,16]{0,1:T(8,128)S(1)}, s32[128,16]{0,1:T(8,128)}, u32[]{:S(2)}) copy-start(s32[128,16]{0,1:T(8,128)} %param.17) | copy-start | bytes 24580
  33.4 10.1 %copy-start.13 = (f32[16,2]{0,1:T(2,128)S(1)}, f32[16,2]{0,1:T(2,128)}, u32[]{:S(2)}) copy-start(f32[16,2]{0,1:T(2,128)} %param.16) | copy-start | bytes 388
  33.4 36.1 %all-to-all-start.1 = ((bf16[16,320,128]{2,1,0:T(8,128)(2,1)}), bf16[16,320,128]{2,1,0:T(8,128)(2,1)S(1)}, u32[]{:S(2)}, u32[]{:S(2)}) async-start(bf16[16,320,128]{2,1,0:T(8,128)(2,1)} %pack.1), calls=%async_computation.1 | async-start | bytes 2621440 | tf_op jit(solution)/shard_map/all_to_all | solution.py:483
  38.7 24.6 %collective-permute-start.2 = (bf16[256,384]{1,0:T(8,128)(2,1)}, bf16[256,384]{1,0:T(8,128)(2,1)}, u32[]{:S(2)}, u32[]{:S(2)}) collective-permute-start(bf16[256,384]{1,0:T(8,128)(2,1)} %pad_maximum_fusion), channel_id=1, source_target_pairs={{0,2},{1,3},{2,4},{3,5},{4,6},{5,7},{6,8},{7,9},{8,10},{9,11},{10,... | collective-permute-start | bytes 589832 | tf_op jit(solution)/shard_map/ppermute | solution.py:25
  45.8 12.5 %collective-permute-start.1 = (bf16[128,384]{1,0:T(8,128)(2,1)S(1)}, bf16[128,384]{1,0:T(8,128)(2,1)S(1)}, u32[]{:S(2)}, u32[]{:S(2)}) collective-permute-start(bf16[128,384]{1,0:T(8,128)(2,1)S(1)} %pair.1.pair_ref), channel_id=1, source_target_pairs={{0,4},{1,5},{2,6},{3,7},{4,8},{5,9},{6,10},{7,11},{8,12},{9,13},{1... | collective-permute-start | bytes 294920 | tf_op jit(solution)/shard_map/ppermute | solution.py:25
  63.3 0.9 %copy-start.5 = (bf16[128,384]{1,0:T(8,128)(2,1)S(1)}, bf16[128,384]{1,0:T(8,128)(2,1)}, u32[]{:S(2)}) copy-start(bf16[128,384]{1,0:T(8,128)(2,1)} %copy-done.4) | copy-start | bytes 294916
  68.5 1.0 %copy-start.10 = (f32[2048,128]{1,0:T(8,128)}, f32[2048,128]{1,0:T(8,128)S(1)}, u32[]{:S(2)}) copy-start(f32[2048,128]{1,0:T(8,128)S(1)} %window.1.win_ref) | copy-start | bytes 3145732
  69.5 7.8 %copy-start.11 = (f32[2048,128]{1,0:T(8,128)S(1)}, f32[2048,128]{1,0:T(8,128)}, u32[]{:S(2)}) copy-start(f32[2048,128]{1,0:T(8,128)} %copy-done.10) | copy-start | bytes 3145732
  69.5 7.7 %collective-permute-start.3 = (bf16[16,320,128]{2,1,0:T(8,128)(2,1)S(1)}, bf16[16,320,128]{2,1,0:T(8,128)(2,1)S(1)}, u32[]{:S(2)}, u32[]{:S(2)}) collective-permute-start(bf16[16,320,128]{2,1,0:T(8,128)(2,1)S(1)} %all-to-all-done.1.kv_ref), channel_id=1, source_target_pairs={{0,16},{16,0},{32,48},{48,32},{64,80},{80,64},{96,112},{112,96},{1... | collective-permute-start | bytes 3932168 | tf_op jit(solution)/shard_map/ppermute | solution.py:486

commit v2 on v1

--- a/solution.py
+++ b/solution.py
@@ -25,21 +25,32 @@
     return lax.ppermute(shard, axis, pairs)
 
 
-def pair_kernel(keys_ref, values_ref, out_ref):
-    out_ref[:, :192] = keys_ref[...].astype(jnp.float32).T.astype(out_ref.dtype)
+def pair_kernel(keys_hbm, values_hbm, out_ref, keys, sems):
+    loads = [
+        pltpu.make_async_copy(keys_hbm, keys, sems.at[0]),
+        pltpu.make_async_copy(values_hbm, out_ref.at[:, 256:], sems.at[1]),
+    ]
+    for load in loads:
+        load.start()
     out_ref[:, 192:256] = jnp.zeros((out_ref.shape[0], 64), out_ref.dtype)
-    out_ref[:, 256:] = values_ref[...]
+    loads[0].wait()
+    out_ref[:, :192] = keys[...].astype(jnp.float32).T.astype(out_ref.dtype)
+    loads[1].wait()
 
 
 def pair(keys, values):
     return pl.pallas_call(
         pair_kernel,
-        in_specs=[pl.BlockSpec(memory_space=pltpu.VMEM)] * 2,
+        in_specs=[pl.BlockSpec(memory_space=pltpu.HBM)] * 2,
         out_specs=pl.BlockSpec(memory_space=pltpu.VMEM),
-        out_shape=jax.ShapeDtypeStruct((keys.shape[0], 384), keys.dtype),
+        out_shape=jax.ShapeDtypeStruct((values.shape[0], 384), keys.dtype),
+        scratch_shapes=[
+            pltpu.VMEM(keys.shape, keys.dtype),
+            pltpu.SemaphoreType.DMA((2,)),
+        ],
         compiler_params=pltpu.CompilerParams(vmem_limit_bytes=GRANT),
         name="pair",
-    )(keys.T, values)
+    )(keys, values)
 
 
 def silu(x):
@@ -57,31 +68,32 @@
     return keys, values
 
 
-def own_kernel(pair_ref, kfirst_ref, vfirst_ref, hidden_ref, wide):
+def own_kernel(
+    pair_ref, kfirst_ref, vfirst_hbm, hidden_ref, kfront_ref, vfront_ref, wide, vback_ref, sems
+):
+    tall = vback_ref.shape[0]
+    loads = [
+        pltpu.make_async_copy(vfirst_hbm.at[tall:], vback_ref, sems.at[0]),
+        pltpu.make_async_copy(vfirst_hbm.at[:tall], vfront_ref, sems.at[1]),
+    ]
+    for load in loads:
+        load.start()
     half_keys = kfirst_ref.shape[1] // 2
-    half_values = vfirst_ref.shape[0] // 2
     count = pair_ref.shape[0] // STRIDE
     for part in range(3):
         lanes = slice(128 * part, 128 * part + 128)
         wide[part] = pair_ref[:, lanes].astype(jnp.float32)
     keys, values = segments(wide, count)
     nothing = jnp.zeros((count, 64), jnp.float32)
-    back = jnp.concatenate(
-        [
-            nt(keys, kfirst_ref[:, half_keys:]),
-            nothing,
-            jnp.dot(values, vfirst_ref[half_values:], preferred_element_type=jnp.float32),
-        ],
-        axis=1,
-    )
-    ahead = jnp.concatenate(
-        [
-            nt(keys, kfirst_ref[:, :half_keys]),
-            nothing,
-            jnp.dot(values, vfirst_ref[:half_values], preferred_element_type=jnp.float32),
-        ],
-        axis=1,
-    )
+    back = nt(keys, kfirst_ref[:, half_keys:])
+    ahead = nt(keys, kfirst_ref[:, :half_keys])
+    kfront_ref[...] = kfirst_ref[:, :half_keys]
+    loads[0].wait()
+    value = jnp.dot(values, vback_ref[...], preferred_element_type=jnp.float32)
+    back = jnp.concatenate([back, nothing, value], axis=1)
+    loads[1].wait()
+    value = jnp.dot(values, vfront_ref[...], preferred_element_type=jnp.float32)
+    ahead = jnp.concatenate([ahead, nothing, value], axis=1)
     row = lax.broadcasted_iota(jnp.int32, back.shape, 0)
     hidden_ref[...] = back + jnp.where(row == 0, 0.0, pltpu.roll(ahead, 1, 0))
 
@@ -91,10 +103,18 @@
     inside = pl.BlockSpec(memory_space=pltpu.VMEM)
     return pl.pallas_call(
         own_kernel,
-        in_specs=[inside] * 3,
-        out_specs=inside,
-        out_shape=jax.ShapeDtypeStruct((rows // STRIDE, 384), jnp.float32),
-        scratch_shapes=[pltpu.VMEM((3, rows, 128), jnp.float32)],
+        in_specs=[inside, inside, pl.BlockSpec(memory_space=pltpu.HBM)],
+        out_specs=[inside] * 3,
+        out_shape=[
+            jax.ShapeDtypeStruct((rows // STRIDE, 384), jnp.float32),
+            jax.ShapeDtypeStruct((kfirst.shape[0], kfirst.shape[1] // 2), kfirst.dtype),
+            jax.ShapeDtypeStruct((vfirst.shape[0] // 2, vfirst.shape[1]), vfirst.dtype),
+        ],
+        scratch_shapes=[
+            pltpu.VMEM((3, rows, 128), jnp.float32),
+            pltpu.VMEM((vfirst.shape[0] // 2, vfirst.shape[1]), vfirst.dtype),
+            pltpu.SemaphoreType.DMA((2,)),
+        ],
         compiler_params=pltpu.CompilerParams(vmem_limit_bytes=GRANT),
         name="own_blocks",
         cost_estimate=pl.CostEstimate(
@@ -104,49 +124,63 @@
 
 
 def summary_kernel(
-    before_ref, hidden_ref, kfirst_ref, ksecond_ref, vfirst_ref, vsecond_ref, out_ref, wide
+    before_ref,
+    hidden_ref,
+    kfront_ref,
+    ksecond_hbm,
+    vfront_ref,
+    vsecond_hbm,
+    out_ref,
+    wide,
+    ksecond,
+    vsecond,
+    sems,
 ):
+    loads = [
+        pltpu.make_async_copy(ksecond_hbm, ksecond, sems.at[0]),
+        pltpu.make_async_copy(vsecond_hbm, vsecond, sems.at[1]),
+    ]
+    for load in loads:
+        load.start()
     rows = before_ref.shape[0]
     count = hidden_ref.shape[0]
     for part in range(3):
         lanes = slice(128 * part, 128 * part + 128)
         wide[part] = before_ref[:, lanes].astype(jnp.float32)
     keys, values = segments(wide, rows // STRIDE)
-    ahead = jnp.concatenate(
-        [
-            nt(keys, kfirst_ref[:, : kfirst_ref.shape[1] // 2]),
-            jnp.zeros((count, 64), jnp.float32),
-            jnp.dot(
-                values,
-                vfirst_ref[: vfirst_ref.shape[0] // 2],
-                preferred_element_type=jnp.float32,
-            ),
-        ],
-        axis=1,
-    )
+    ahead = nt(keys, kfront_ref[...])
+    value = jnp.dot(values, vfront_ref[...], preferred_element_type=jnp.float32)
+    ahead = jnp.concatenate([ahead, jnp.zeros((count, 64), jnp.float32), value], axis=1)
     row = lax.broadcasted_iota(jnp.int32, ahead.shape, 0)
     hidden = hidden_ref[...] + jnp.where(row == 0, pltpu.roll(ahead, 1, 0), 0.0)
     hidden = silu(hidden).astype(jnp.bfloat16)
-    key = jnp.dot(hidden[:, :192], ksecond_ref[...], preferred_element_type=jnp.float32)
-    value = jnp.dot(hidden[:, 256:], vsecond_ref[...], preferred_element_type=jnp.float32)
+    for load in loads:
+        load.wait()
+    key = jnp.dot(hidden[:, :192], ksecond[...], preferred_element_type=jnp.float32)
+    value = jnp.dot(hidden[:, 256:], vsecond[...], preferred_element_type=jnp.float32)
     high = jnp.concatenate([key[:, 128:], jnp.zeros((count, 64), jnp.float32)], axis=1)
     payload = jnp.concatenate([key[:, :128], high, value], axis=0).astype(out_ref.dtype)
     for copy in range(out_ref.shape[0]):
         out_ref[copy] = payload
 
 
-def summary(before, hidden, kfirst, key_second, vfirst, value_second, copies):
+def summary(before, hidden, kfront, key_second, vfront, value_second, copies):
     inside = pl.BlockSpec(memory_space=pltpu.VMEM)
-    default = pl.BlockSpec()
+    outside = pl.BlockSpec(memory_space=pltpu.HBM)
     return pl.pallas_call(
         summary_kernel,
-        in_specs=[inside, inside, inside, default, inside, default],
+        in_specs=[inside, inside, inside, outside, inside, outside],
         out_specs=inside,
         out_shape=jax.ShapeDtypeStruct((copies, 3 * hidden.shape[0], 128), jnp.bfloat16),
-        scratch_shapes=[pltpu.VMEM((3,) + (before.shape[0], 128), jnp.float32)],
+        scratch_shapes=[
+            pltpu.VMEM((3,) + (before.shape[0], 128), jnp.float32),
+            pltpu.VMEM(key_second.shape, jnp.bfloat16),
+            pltpu.VMEM(value_second.shape, jnp.bfloat16),
+            pltpu.SemaphoreType.DMA((2,)),
+        ],
         compiler_params=pltpu.CompilerParams(vmem_limit_bytes=GRANT),
         name="summary",
-    )(before, hidden, kfirst, key_second, vfirst, value_second)
+    )(before, hidden, kfront, key_second, vfront, value_second)
 
 
 def pack_kernel(column_ref, out_hbm, packed, sems):
@@ -463,11 +497,17 @@
     who = jnp.stack([device, core, outer // 2]).astype(jnp.int32)
     planes = lax.axis_size("sa") // 2
     scale = depth ** (-0.5)
-    paired = pair(keys, values)
+
+    def stay(x):
+        return pltpu.with_memory_space_constraint(x, pltpu.HBM)
+
+    paired = pair(stay(keys.T), stay(values))
     one = shifted(paired, ("sa", "sb"), 1)
     kfirst = key_first.T
-    hidden = own_blocks(paired, kfirst, value_first)
-    payload = summary(one, hidden, kfirst, key_second, value_first, value_second, planes)
+    hidden, kfront, vfront = own_blocks(paired, kfirst, stay(value_first))
+    payload = summary(
+        one, hidden, kfront, stay(key_second), vfront, stay(value_second), planes
+    )
     payload, later, again = lax.optimization_barrier((payload, one, paired))
     groups = [[2 * z + c for z in range(planes)] for c in range(2)]
     column = lax.all_to_all(payload, "sa", 0, 0, axis_index_groups=groups)

time: 85.9 us -> 84.6 us (0.985)
  local copies, waits for them, and re-layouts: 8.69 us -> 5.89 us
  Pallas kernels: 20 us -> 21.8 us
  waiting for transfers between devices: 18.1 us -> 19.3 us
    unnamed x30 -> x16, local copies, waits for them, and re-layouts: 8.24 us -> 5.44 us
    pallas_call x3, Pallas kernels: 1.69 us -> 3.56 us  [the longest x1 1.57 us: own_blocks(): pl.pallas_call(own_kernel, in_specs=[inside, inside, pl.BlockSpec(memory_...]
    ppermute x3, waiting for transfers between devices: 18.1 us -> 19.3 us  [shifted(): return lax.ppermute(shard, axis, pairs)]
  transfers between devices with their start and end apart: 5 -> 5, of which waited for: 3 -> 3; matrix products, arithmetic and copies ran while one was open for 4% -> 4% of each run, Pallas kernels for 13% -> 14%
where the time goes in v2:
time: 84.6 us; the launch traced here: 83.9 us
  Pallas kernels  21.8 us (26%)
  waiting for transfers between devices  19.3 us (23%)
  blocking collectives  18.9 us (22%)
  starting transfers between devices  16.7 us (20%)
  local copies, waits for them, and re-layouts  5.89 us (7%)
  other arithmetic  0.92 us (1%)
    ppermute x3, waiting for transfers between devices, shifted(): return lax.ppermute(shard, axis, pairs)  19.3 us
    all_to_all x1, blocking collectives, local(): column = lax.all_to_all(payload, 'sa', 0, 0, axis_index_groups=groups)  18.9 us
    ppermute x3, starting transfers between devices, shifted(): return lax.ppermute(shard, axis, pairs)  11 us
    pallas_call x1, Pallas kernels, second_half(): pl.pallas_call(functools.partial(second_kernel, scale, heads), in_specs=[...  6.97 us
    pallas_call x1, Pallas kernels, first_half(): pl.pallas_call(functools.partial(first_kernel, scale, heads), in_specs=[p...  5.69 us
    unnamed x16, local copies, waits for them, and re-layouts  5.44 us
    pallas_call x1, Pallas kernels, window_branch(): pl.pallas_call(functools.partial(window_kernel, scale, heads), grid_spec=...  4.3 us
    all_to_all x1, starting transfers between devices, local(): mine = lax.all_to_all(copies, 'sb', 0, 0)  3.71 us
  transfers between devices with their start and end apart: 5, of which 3 were waited for; matrix products, arithmetic and copies ran while one was open for 4% of the time, Pallas kernels for 14%

profile of v2, /device:TPU:481, one launch (start us, length us, event | category | flops | bytes accessed | tf_op | source)
XLA Modules:
  0.0 83.9 jit_solution(17876421769288703387)
XLA Ops:
  0.0 0.9 %pair.1.pair_ref = bf16[128,384]{1,0:T(8,128)(2,1)S(1)} custom-call(bf16[192,128]{1,0:T(8,128)(2,1)} %bitcast.11, bf16[128,128]{1,0:T(8,128)(2,1)} %values_hbm.1), custom_call_target="tpu_custom_call" | custom-call | tf_op jit(solution)/shard_map/pair/pallas_call | solution.py:42
  0.9 0.0 copy-start
  0.9 3.2 %collective-permute-start = (bf16[128,384]{1,0:T(8,128)(2,1)S(1)}, bf16[128,384]{1,0:T(8,128)(2,1)S(1)}, u32[]{:S(2)}, u32[]{:S(2)}) collective-permute-start(bf16[128,384]{1,0:T(8,128)(2,1)S(1)} %pair.1.pair_ref), channel_id=1, source_target_pairs={{0,1},{1,2},{2,3},{3,4},{4,5},{5,6},{6,7},{7,8},{8,9},{9,10},{10,1... | collective-permute-start | bytes 294920 | tf_op jit(solution)/shard_map/ppermute | solution.py:25
  4.2 0.0 copy-start.2
  4.2 1.7 %copy-done.2 = bf16[6144,192]{0,1:T(8,128)(2,1)S(1)} copy-done((bf16[6144,192]{0,1:T(8,128)(2,1)S(1)}, bf16[6144,192]{0,1:T(8,128)(2,1)}, u32[]{:S(2)}) %copy-start.2) | copy-done | bytes 2359320
  5.8 1.6 %own_blocks.1 = (f32[8,384]{1,0:T(8,128)S(1)}, bf16[192,3072]{1,0:T(8,128)(2,1)S(1)}, bf16[2048,128]{1,0:T(8,128)(2,1)S(1)}) custom-call(bf16[128,384]{1,0:T(8,128)(2,1)S(1)} %pair.1.pair_ref, bf16[192,6144]{1,0:T(8,128)(2,1)S(1)} %bitcast.10, bf16[4096,128]{1,0:T(8,128)(2,1)} %vfirst_hbm.1), custom_call_target="tpu_custom_call" | custom-call | flops 1000000000 | bytes 8000000 | tf_op jit(solution)/shard_map/own_blocks/pallas_call | solution.py:104
  7.4 4.3 %collective-permute-done.before_ref.one_ref = bf16[128,384]{1,0:T(8,128)(2,1)S(1)} collective-permute-done((bf16[128,384]{1,0:T(8,128)(2,1)S(1)}, bf16[128,384]{1,0:T(8,128)(2,1)S(1)}, u32[]{:S(2)}, u32[]{:S(2)}) %collective-permute-start) | collective-permute-done | bytes 98336 | tf_op jit(solution)/shard_map/ppermute | solution.py:25
  11.7 1.1 %summary.1 = bf16[16,24,128]{2,1,0:T(8,128)(2,1)S(1)} custom-call(bf16[128,384]{1,0:T(8,128)(2,1)S(1)} %collective-permute-done.before_ref.one_ref, f32[8,384]{1,0:T(8,128)S(1)} %get-tuple-element.15.hidden_ref, bf16[192,3072]{1,0:T(8,128)(2,1)S(1)} %get-tuple-element.16.kfront_ref, bf16[192,192]{1,0:T(8,128)(2,1)} %ksecond_hbm.1, ...), custom_call_target="tpu_custom_call" | custom-call | tf_op jit(solution)/shard_map/summary/pallas_call | solution.py:170
  12.8 18.9 %all_to_all.10.column_ref = bf16[16,24,128]{2,1,0:T(8,128)(2,1)S(1)} all-to-all(bf16[16,24,128]{2,1,0:T(8,128)(2,1)S(1)} %summary.1), channel_id=1, replica_groups={{0,32,64,96,128,160,192,224,256,288,320,352,384,416,448,480},{16,48,80,..., dimensions={0} | all-to-all | bytes 196608 | tf_op jit(solution)/shard_map/all_to_all | solution.py:513
  31.7 1.3 %pack.1 = bf16[16,320,128]{2,1,0:T(8,128)(2,1)} custom-call(bf16[16,24,128]{2,1,0:T(8,128)(2,1)S(1)} %all_to_all.10.column_ref), custom_call_target="tpu_custom_call" | custom-call | tf_op jit(solution)/shard_map/pack/pallas_call | solution.py:214
  33.0 0.0 copy-start.5
  33.0 0.0 copy-start.6
  33.0 3.7 %all-to-all-start.1 = ((bf16[16,320,128]{2,1,0:T(8,128)(2,1)}), bf16[16,320,128]{2,1,0:T(8,128)(2,1)S(1)}, u32[]{:S(2)}, u32[]{:S(2)}) async-start(bf16[16,320,128]{2,1,0:T(8,128)(2,1)} %pack.1), calls=%async_computation.1 | async-start | bytes 2621440 | tf_op jit(solution)/shard_map/all_to_all | solution.py:523
  36.7 0.0 copy-done.5
  36.8 0.1 copy.16
  36.9 0.1 eq.21
  37.0 0.0 copy-done
  37.0 0.7 pad_maximum_fusion
  37.7 4.6 %collective-permute-start.2 = (bf16[256,384]{1,0:T(8,128)(2,1)}, bf16[256,384]{1,0:T(8,128)(2,1)}, u32[]{:S(2)}, u32[]{:S(2)}) collective-permute-start(bf16[256,384]{1,0:T(8,128)(2,1)} %pad_maximum_fusion), channel_id=1, source_target_pairs={{0,2},{1,3},{2,4},{3,5},{4,6},{5,7},{6,8},{7,9},{8,10},{9,11},{10,... | collective-permute-start | bytes 589832 | tf_op jit(solution)/shard_map/ppermute | solution.py:25
  42.3 0.0 copy-done.6
  42.3 0.1 multiply_reduce_fusion
  42.5 0.4 copy.17.gate_ref
  42.8 1.8 %copy.15 = bf16[128,16,192]{2,1,0:T(8,128)(2,1)S(1)} copy(bf16[128,16,192]{0,2,1:T(8,128)(2,1)} %param.9) | data formatting | bytes 1572864 | tf_op args[0]
  44.7 3.1 %collective-permute-start.1 = (bf16[128,384]{1,0:T(8,128)(2,1)}, bf16[128,384]{1,0:T(8,128)(2,1)S(1)}, u32[]{:S(2)}, u32[]{:S(2)}) collective-permute-start(bf16[128,384]{1,0:T(8,128)(2,1)} %copy-done), channel_id=1, source_target_pairs={{0,4},{1,5},{2,6},{3,7},{4,8},{5,9},{6,10},{7,11},{8,12},{9,13},{1... | collective-permute-start | bytes 294920 | tf_op jit(solution)/shard_map/ppermute | solution.py:25
  47.8 0.1 pad_add_fusion.who
  47.9 9.8 %collective-permute-done.1.four_ref = bf16[128,384]{1,0:T(8,128)(2,1)S(1)} collective-permute-done((bf16[128,384]{1,0:T(8,128)(2,1)}, bf16[128,384]{1,0:T(8,128)(2,1)S(1)}, u32[]{:S(2)}, u32[]{:S(2)}) %collective-permute-start.1) | collective-permute-done | bytes 98336 | tf_op jit(solution)/shard_map/ppermute | solution.py:25
  57.7 5.2 %collective-permute-done.2.two_ref = bf16[256,384]{1,0:T(8,128)(2,1)} collective-permute-done((bf16[256,384]{1,0:T(8,128)(2,1)}, bf16[256,384]{1,0:T(8,128)(2,1)}, u32[]{:S(2)}, u32[]{:S(2)}) %collective-permute-start.2) | collective-permute-done | bytes 196640 | tf_op jit(solution)/shard_map/ppermute | solution.py:25
  62.8 0.0 copy-start.1
  62.8 0.9 %copy-done.1 = bf16[128,384]{1,0:T(8,128)(2,1)S(1)} copy-done((bf16[128,384]{1,0:T(8,128)(2,1)S(1)}, bf16[128,384]{1,0:T(8,128)(2,1)}, u32[]{:S(2)}) %copy-start.1) | copy-done | bytes 98328
  63.7 4.3 %window.1.win_ref = f32[2048,128]{1,0:T(8,128)S(1)} custom-call(s32[3]{0:T(128)S(1)} %pad_add_fusion.who, bf16[2048,192]{1,0:T(8,128)(2,1)S(1)} %bitcast.7, bf16[128,384]{1,0:T(8,128)(2,1)S(1)} %collective-permute-done.1.four_ref, bf16[256,384]{1,0:T(8,128)(2,1)} %collective-permute-done.2.two_ref, ...), custom_call_target="tpu_custom_call" | custom-call | flops 1342177280 | bytes 4000000 | tf_op jit(solution)/shard_map/window/pallas_call | solution.py:291
  68.0 0.0 copy-start.3
  68.1 0.9 %copy-done.3 = f32[2048,128]{1,0:T(8,128)} copy-done((f32[2048,128]{1,0:T(8,128)}, f32[2048,128]{1,0:T(8,128)S(1)}, u32[]{:S(2)}) %copy-start.3) | copy-done | bytes 1048600
  69.0 0.0 all-to-all-done.1.kv_ref
  69.0 0.0 copy-start.4
  69.0 2.0 %collective-permute-start.3 = (bf16[16,320,128]{2,1,0:T(8,128)(2,1)S(1)}, bf16[16,320,128]{2,1,0:T(8,128)(2,1)S(1)}, u32[]{:S(2)}, u32[]{:S(2)}) collective-permute-start(bf16[16,320,128]{2,1,0:T(8,128)(2,1)S(1)} %all-to-all-done.1.kv_ref), channel_id=1, source_target_pairs={{0,16},{16,0},{32,48},{48,32},{64,80},{80,64},{96,112},{112,96},{1... | collective-permute-start | bytes 3932168 | tf_op jit(solution)/shard_map/ppermute | solution.py:526
  71.1 5.7 %first_half.1 = (f32[2048,256]{1,0:T(8,128)S(1)}, f32[2048,128]{1,0:T(8,128)S(1)}) custom-call(s32[3]{0:T(128)S(1)} %pad_add_fusion.who, bf16[2048,192]{1,0:T(8,128)(2,1)S(1)} %bitcast.8, bf16[16,320,128]{2,1,0:T(8,128)(2,1)S(1)} %all-to-all-done.1.kv_ref), custom_call_target="tpu_custom_call" | custom-call | flops 4294967296 | bytes 3000000 | tf_op jit(solution)/shard_map/first_half/pallas_call | solution.py:450
  76.8 0.0 collective-permute-done.3.kv_ref
  76.8 0.0 copy-done.4
  76.8 7.0 %second_half.1 = bf16[2048,128]{1,0:T(8,128)(2,1)} custom-call(s32[3]{0:T(128)S(1)} %pad_add_fusion.who, bf16[2048,192]{1,0:T(8,128)(2,1)S(1)} %bitcast.9, bf16[16,320,128]{2,1,0:T(8,128)(2,1)S(1)} %collective-permute-done.3.kv_ref, f32[2048,256]{1,0:T(8,128)S(1)} %get-tuple-element.22.acc_ref, f32[2048,128]{1,0:T(8,128)S(1)} %get-tuple-element.23.top_ref, ...), custom_call_target="tpu_custom_call" | custom-call | flops 4294967296 | bytes 5000000 | tf_op jit(solution)/shard_map/second_half/pallas_call | solution.py:471
  (1 shorter events, 0.0 us)
Async XLA Ops:
  0.9 36.0 %copy-start = (bf16[128,384]{1,0:T(8,128)(2,1)}, bf16[128,384]{1,0:T(8,128)(2,1)S(1)}, u32[]{:S(2)}) copy-start(bf16[128,384]{1,0:T(8,128)(2,1)S(1)} %pair.1.pair_ref) | copy-start | bytes 294916
  0.9 10.7 %collective-permute-start = (bf16[128,384]{1,0:T(8,128)(2,1)S(1)}, bf16[128,384]{1,0:T(8,128)(2,1)S(1)}, u32[]{:S(2)}, u32[]{:S(2)}) collective-permute-start(bf16[128,384]{1,0:T(8,128)(2,1)S(1)} %pair.1.pair_ref), channel_id=1, source_target_pairs={{0,1},{1,2},{2,3},{3,4},{4,5},{5,6},{6,7},{7,8},{8,9},{9,10},{10,1... | collective-permute-start | bytes 294920 | tf_op jit(solution)/shard_map/ppermute | solution.py:25
  4.2 1.7 %copy-start.2 = (bf16[6144,192]{0,1:T(8,128)(2,1)S(1)}, bf16[6144,192]{0,1:T(8,128)(2,1)}, u32[]{:S(2)}) copy-start(bf16[6144,192]{0,1:T(8,128)(2,1)} %param.12) | copy-start | bytes 7077892
  33.0 3.8 %copy-start.5 = (s32[128,16]{0,1:T(8,128)S(1)}, s32[128,16]{0,1:T(8,128)}, u32[]{:S(2)}) copy-start(s32[128,16]{0,1:T(8,128)} %param.17) | copy-start | bytes 24580
  33.0 9.3 %copy-start.6 = (f32[16,2]{0,1:T(2,128)S(1)}, f32[16,2]{0,1:T(2,128)}, u32[]{:S(2)}) copy-start(f32[16,2]{0,1:T(2,128)} %param.16) | copy-start | bytes 388
  33.0 36.0 %all-to-all-start.1 = ((bf16[16,320,128]{2,1,0:T(8,128)(2,1)}), bf16[16,320,128]{2,1,0:T(8,128)(2,1)S(1)}, u32[]{:S(2)}, u32[]{:S(2)}) async-start(bf16[16,320,128]{2,1,0:T(8,128)(2,1)} %pack.1), calls=%async_computation.1 | async-start | bytes 2621440 | tf_op jit(solution)/shard_map/all_to_all | solution.py:523
  37.7 25.2 %collective-permute-start.2 = (bf16[256,384]{1,0:T(8,128)(2,1)}, bf16[256,384]{1,0:T(8,128)(2,1)}, u32[]{:S(2)}, u32[]{:S(2)}) collective-permute-start(bf16[256,384]{1,0:T(8,128)(2,1)} %pad_maximum_fusion), channel_id=1, source_target_pairs={{0,2},{1,3},{2,4},{3,5},{4,6},{5,7},{6,8},{7,9},{8,10},{9,11},{10,... | collective-permute-start | bytes 589832 | tf_op jit(solution)/shard_map/ppermute | solution.py:25
  44.7 13.0 %collective-permute-start.1 = (bf16[128,384]{1,0:T(8,128)(2,1)}, bf16[128,384]{1,0:T(8,128)(2,1)S(1)}, u32[]{:S(2)}, u32[]{:S(2)}) collective-permute-start(bf16[128,384]{1,0:T(8,128)(2,1)} %copy-done), channel_id=1, source_target_pairs={{0,4},{1,5},{2,6},{3,7},{4,8},{5,9},{6,10},{7,11},{8,12},{9,13},{1... | collective-permute-start | bytes 294920 | tf_op jit(solution)/shard_map/ppermute | solution.py:25
  62.8 0.9 %copy-start.1 = (bf16[128,384]{1,0:T(8,128)(2,1)S(1)}, bf16[128,384]{1,0:T(8,128)(2,1)}, u32[]{:S(2)}) copy-start(bf16[128,384]{1,0:T(8,128)(2,1)} %copy-done) | copy-start | bytes 294916
  68.0 1.0 %copy-start.3 = (f32[2048,128]{1,0:T(8,128)}, f32[2048,128]{1,0:T(8,128)S(1)}, u32[]{:S(2)}) copy-start(f32[2048,128]{1,0:T(8,128)S(1)} %window.1.win_ref) | copy-start | bytes 3145732
  69.0 7.8 %copy-start.4 = (f32[2048,128]{1,0:T(8,128)S(1)}, f32[2048,128]{1,0:T(8,128)}, u32[]{:S(2)}) copy-start(f32[2048,128]{1,0:T(8,128)} %copy-done.3) | copy-start | bytes 3145732
  69.0 7.7 %collective-permute-start.3 = (bf16[16,320,128]{2,1,0:T(8,128)(2,1)S(1)}, bf16[16,320,128]{2,1,0:T(8,128)(2,1)S(1)}, u32[]{:S(2)}, u32[]{:S(2)}) collective-permute-start(bf16[16,320,128]{2,1,0:T(8,128)(2,1)S(1)} %all-to-all-done.1.kv_ref), channel_id=1, source_target_pairs={{0,16},{16,0},{32,48},{48,32},{64,80},{80,64},{96,112},{112,96},{1... | collective-permute-start | bytes 3932168 | tf_op jit(solution)/shard_map/ppermute | solution.py:526

commit v3 on v2

--- a/solution.py
+++ b/solution.py
@@ -387,11 +387,11 @@
     def _():
         run(1)
 
-    @pl.when((plane >= 4) & (plane < 8))
+    @pl.when((plane >= 4) & (plane < 12))
     def _():
-        run(2)
-
-    @pl.when(plane >= 8)
+        run(3)
+
+    @pl.when(plane >= 12)
     def _():
         run(4)
 

time: 84.6 us -> 84.6 us (level)
  no operation moved by 1% of the time
where the time goes in v3:
time: 84.6 us; the launch traced here: 83.9 us
  Pallas kernels  21.8 us (26%)
  waiting for transfers between devices  19.3 us (23%)
  blocking collectives  18.9 us (22%)
  starting transfers between devices  16.7 us (20%)
  local copies, waits for them, and re-layouts  5.89 us (7%)
  other arithmetic  0.92 us (1%)
    ppermute x3, waiting for transfers between devices, shifted(): return lax.ppermute(shard, axis, pairs)  19.3 us
    all_to_all x1, blocking collectives, local(): column = lax.all_to_all(payload, 'sa', 0, 0, axis_index_groups=groups)  18.9 us
    ppermute x3, starting transfers between devices, shifted(): return lax.ppermute(shard, axis, pairs)  11 us
    pallas_call x1, Pallas kernels, second_half(): pl.pallas_call(functools.partial(second_kernel, scale, heads), in_specs=[...  6.98 us
    pallas_call x1, Pallas kernels, first_half(): pl.pallas_call(functools.partial(first_kernel, scale, heads), in_specs=[p...  5.69 us
    unnamed x16, local copies, waits for them, and re-layouts  5.44 us
    pallas_call x1, Pallas kernels, window_branch(): pl.pallas_call(functools.partial(window_kernel, scale, heads), grid_spec=...  4.3 us
    all_to_all x1, starting transfers between devices, local(): mine = lax.all_to_all(copies, 'sb', 0, 0)  3.71 us
  transfers between devices with their start and end apart: 5, of which 3 were waited for; matrix products, arithmetic and copies ran while one was open for 4% of the time, Pallas kernels for 14%

profile of v3, /device:TPU:481, one launch (start us, length us, event | category | flops | bytes accessed | tf_op | source)
XLA Modules:
  0.0 83.9 jit_solution(7250637118941885911)
XLA Ops:
  0.0 0.9 %pair.1.pair_ref = bf16[128,384]{1,0:T(8,128)(2,1)S(1)} custom-call(bf16[192,128]{1,0:T(8,128)(2,1)} %bitcast.11, bf16[128,128]{1,0:T(8,128)(2,1)} %values_hbm.1), custom_call_target="tpu_custom_call" | custom-call | tf_op jit(solution)/shard_map/pair/pallas_call | solution.py:42
  0.9 0.0 copy-start
  0.9 3.2 %collective-permute-start = (bf16[128,384]{1,0:T(8,128)(2,1)S(1)}, bf16[128,384]{1,0:T(8,128)(2,1)S(1)}, u32[]{:S(2)}, u32[]{:S(2)}) collective-permute-start(bf16[128,384]{1,0:T(8,128)(2,1)S(1)} %pair.1.pair_ref), channel_id=1, source_target_pairs={{0,1},{1,2},{2,3},{3,4},{4,5},{5,6},{6,7},{7,8},{8,9},{9,10},{10,1... | collective-permute-start | bytes 294920 | tf_op jit(solution)/shard_map/ppermute | solution.py:25
  4.2 0.0 copy-start.2
  4.2 1.7 %copy-done.2 = bf16[6144,192]{0,1:T(8,128)(2,1)S(1)} copy-done((bf16[6144,192]{0,1:T(8,128)(2,1)S(1)}, bf16[6144,192]{0,1:T(8,128)(2,1)}, u32[]{:S(2)}) %copy-start.2) | copy-done | bytes 2359320
  5.8 1.6 %own_blocks.1 = (f32[8,384]{1,0:T(8,128)S(1)}, bf16[192,3072]{1,0:T(8,128)(2,1)S(1)}, bf16[2048,128]{1,0:T(8,128)(2,1)S(1)}) custom-call(bf16[128,384]{1,0:T(8,128)(2,1)S(1)} %pair.1.pair_ref, bf16[192,6144]{1,0:T(8,128)(2,1)S(1)} %bitcast.10, bf16[4096,128]{1,0:T(8,128)(2,1)} %vfirst_hbm.1), custom_call_target="tpu_custom_call" | custom-call | flops 1000000000 | bytes 8000000 | tf_op jit(solution)/shard_map/own_blocks/pallas_call | solution.py:104
  7.4 4.3 %collective-permute-done.before_ref.one_ref = bf16[128,384]{1,0:T(8,128)(2,1)S(1)} collective-permute-done((bf16[128,384]{1,0:T(8,128)(2,1)S(1)}, bf16[128,384]{1,0:T(8,128)(2,1)S(1)}, u32[]{:S(2)}, u32[]{:S(2)}) %collective-permute-start) | collective-permute-done | bytes 98336 | tf_op jit(solution)/shard_map/ppermute | solution.py:25
  11.7 1.1 %summary.1 = bf16[16,24,128]{2,1,0:T(8,128)(2,1)S(1)} custom-call(bf16[128,384]{1,0:T(8,128)(2,1)S(1)} %collective-permute-done.before_ref.one_ref, f32[8,384]{1,0:T(8,128)S(1)} %get-tuple-element.15.hidden_ref, bf16[192,3072]{1,0:T(8,128)(2,1)S(1)} %get-tuple-element.16.kfront_ref, bf16[192,192]{1,0:T(8,128)(2,1)} %ksecond_hbm.1, ...), custom_call_target="tpu_custom_call" | custom-call | tf_op jit(solution)/shard_map/summary/pallas_call | solution.py:170
  12.8 18.9 %all_to_all.10.column_ref = bf16[16,24,128]{2,1,0:T(8,128)(2,1)S(1)} all-to-all(bf16[16,24,128]{2,1,0:T(8,128)(2,1)S(1)} %summary.1), channel_id=1, replica_groups={{0,32,64,96,128,160,192,224,256,288,320,352,384,416,448,480},{16,48,80,..., dimensions={0} | all-to-all | bytes 196608 | tf_op jit(solution)/shard_map/all_to_all | solution.py:513
  31.7 1.3 %pack.1 = bf16[16,320,128]{2,1,0:T(8,128)(2,1)} custom-call(bf16[16,24,128]{2,1,0:T(8,128)(2,1)S(1)} %all_to_all.10.column_ref), custom_call_target="tpu_custom_call" | custom-call | tf_op jit(solution)/shard_map/pack/pallas_call | solution.py:214
  33.0 0.0 copy-start.5
  33.0 0.0 copy-start.6
  33.0 3.7 %all-to-all-start.1 = ((bf16[16,320,128]{2,1,0:T(8,128)(2,1)}), bf16[16,320,128]{2,1,0:T(8,128)(2,1)S(1)}, u32[]{:S(2)}, u32[]{:S(2)}) async-start(bf16[16,320,128]{2,1,0:T(8,128)(2,1)} %pack.1), calls=%async_computation.1 | async-start | bytes 2621440 | tf_op jit(solution)/shard_map/all_to_all | solution.py:523
  36.7 0.0 copy-done.5
  36.8 0.1 copy.16
  36.9 0.1 eq.21
  37.0 0.0 copy-done
  37.0 0.7 pad_maximum_fusion
  37.7 4.6 %collective-permute-start.2 = (bf16[256,384]{1,0:T(8,128)(2,1)}, bf16[256,384]{1,0:T(8,128)(2,1)}, u32[]{:S(2)}, u32[]{:S(2)}) collective-permute-start(bf16[256,384]{1,0:T(8,128)(2,1)} %pad_maximum_fusion), channel_id=1, source_target_pairs={{0,2},{1,3},{2,4},{3,5},{4,6},{5,7},{6,8},{7,9},{8,10},{9,11},{10,... | collective-permute-start | bytes 589832 | tf_op jit(solution)/shard_map/ppermute | solution.py:25
  42.3 0.0 copy-done.6
  42.3 0.1 multiply_reduce_fusion
  42.5 0.4 copy.17.gate_ref
  42.8 1.8 %copy.15 = bf16[128,16,192]{2,1,0:T(8,128)(2,1)S(1)} copy(bf16[128,16,192]{0,2,1:T(8,128)(2,1)} %param.9) | data formatting | bytes 1572864 | tf_op args[0]
  44.7 3.1 %collective-permute-start.1 = (bf16[128,384]{1,0:T(8,128)(2,1)}, bf16[128,384]{1,0:T(8,128)(2,1)S(1)}, u32[]{:S(2)}, u32[]{:S(2)}) collective-permute-start(bf16[128,384]{1,0:T(8,128)(2,1)} %copy-done), channel_id=1, source_target_pairs={{0,4},{1,5},{2,6},{3,7},{4,8},{5,9},{6,10},{7,11},{8,12},{9,13},{1... | collective-permute-start | bytes 294920 | tf_op jit(solution)/shard_map/ppermute | solution.py:25
  47.8 0.1 pad_add_fusion.who
  47.9 9.8 %collective-permute-done.1.four_ref = bf16[128,384]{1,0:T(8,128)(2,1)S(1)} collective-permute-done((bf16[128,384]{1,0:T(8,128)(2,1)}, bf16[128,384]{1,0:T(8,128)(2,1)S(1)}, u32[]{:S(2)}, u32[]{:S(2)}) %collective-permute-start.1) | collective-permute-done | bytes 98336 | tf_op jit(solution)/shard_map/ppermute | solution.py:25
  57.7 5.2 %collective-permute-done.2.two_ref = bf16[256,384]{1,0:T(8,128)(2,1)} collective-permute-done((bf16[256,384]{1,0:T(8,128)(2,1)}, bf16[256,384]{1,0:T(8,128)(2,1)}, u32[]{:S(2)}, u32[]{:S(2)}) %collective-permute-start.2) | collective-permute-done | bytes 196640 | tf_op jit(solution)/shard_map/ppermute | solution.py:25
  62.8 0.0 copy-start.1
  62.8 0.9 %copy-done.1 = bf16[128,384]{1,0:T(8,128)(2,1)S(1)} copy-done((bf16[128,384]{1,0:T(8,128)(2,1)S(1)}, bf16[128,384]{1,0:T(8,128)(2,1)}, u32[]{:S(2)}) %copy-start.1) | copy-done | bytes 98328
  63.7 4.3 %window.1.win_ref = f32[2048,128]{1,0:T(8,128)S(1)} custom-call(s32[3]{0:T(128)S(1)} %pad_add_fusion.who, bf16[2048,192]{1,0:T(8,128)(2,1)S(1)} %bitcast.7, bf16[128,384]{1,0:T(8,128)(2,1)S(1)} %collective-permute-done.1.four_ref, bf16[256,384]{1,0:T(8,128)(2,1)} %collective-permute-done.2.two_ref, ...), custom_call_target="tpu_custom_call" | custom-call | flops 1342177280 | bytes 4000000 | tf_op jit(solution)/shard_map/window/pallas_call | solution.py:291
  68.0 0.0 copy-start.3
  68.1 0.9 %copy-done.3 = f32[2048,128]{1,0:T(8,128)} copy-done((f32[2048,128]{1,0:T(8,128)}, f32[2048,128]{1,0:T(8,128)S(1)}, u32[]{:S(2)}) %copy-start.3) | copy-done | bytes 1048600
  69.0 0.0 all-to-all-done.1.kv_ref
  69.0 0.0 copy-start.4
  69.0 2.0 %collective-permute-start.3 = (bf16[16,320,128]{2,1,0:T(8,128)(2,1)S(1)}, bf16[16,320,128]{2,1,0:T(8,128)(2,1)S(1)}, u32[]{:S(2)}, u32[]{:S(2)}) collective-permute-start(bf16[16,320,128]{2,1,0:T(8,128)(2,1)S(1)} %all-to-all-done.1.kv_ref), channel_id=1, source_target_pairs={{0,16},{16,0},{32,48},{48,32},{64,80},{80,64},{96,112},{112,96},{1... | collective-permute-start | bytes 3932168 | tf_op jit(solution)/shard_map/ppermute | solution.py:526
  71.1 5.7 %first_half.1 = (f32[2048,256]{1,0:T(8,128)S(1)}, f32[2048,128]{1,0:T(8,128)S(1)}) custom-call(s32[3]{0:T(128)S(1)} %pad_add_fusion.who, bf16[2048,192]{1,0:T(8,128)(2,1)S(1)} %bitcast.8, bf16[16,320,128]{2,1,0:T(8,128)(2,1)S(1)} %all-to-all-done.1.kv_ref), custom_call_target="tpu_custom_call" | custom-call | flops 4294967296 | bytes 3000000 | tf_op jit(solution)/shard_map/first_half/pallas_call | solution.py:450
  76.8 0.0 collective-permute-done.3.kv_ref
  76.8 0.0 copy-done.4
  76.8 7.0 %second_half.1 = bf16[2048,128]{1,0:T(8,128)(2,1)} custom-call(s32[3]{0:T(128)S(1)} %pad_add_fusion.who, bf16[2048,192]{1,0:T(8,128)(2,1)S(1)} %bitcast.9, bf16[16,320,128]{2,1,0:T(8,128)(2,1)S(1)} %collective-permute-done.3.kv_ref, f32[2048,256]{1,0:T(8,128)S(1)} %get-tuple-element.22.acc_ref, f32[2048,128]{1,0:T(8,128)S(1)} %get-tuple-element.23.top_ref, ...), custom_call_target="tpu_custom_call" | custom-call | flops 4294967296 | bytes 5000000 | tf_op jit(solution)/shard_map/second_half/pallas_call | solution.py:471
  (1 shorter events, 0.0 us)
Async XLA Ops:
  0.9 36.0 %copy-start = (bf16[128,384]{1,0:T(8,128)(2,1)}, bf16[128,384]{1,0:T(8,128)(2,1)S(1)}, u32[]{:S(2)}) copy-start(bf16[128,384]{1,0:T(8,128)(2,1)S(1)} %pair.1.pair_ref) | copy-start | bytes 294916
  0.9 10.7 %collective-permute-start = (bf16[128,384]{1,0:T(8,128)(2,1)S(1)}, bf16[128,384]{1,0:T(8,128)(2,1)S(1)}, u32[]{:S(2)}, u32[]{:S(2)}) collective-permute-start(bf16[128,384]{1,0:T(8,128)(2,1)S(1)} %pair.1.pair_ref), channel_id=1, source_target_pairs={{0,1},{1,2},{2,3},{3,4},{4,5},{5,6},{6,7},{7,8},{8,9},{9,10},{10,1... | collective-permute-start | bytes 294920 | tf_op jit(solution)/shard_map/ppermute | solution.py:25
  4.2 1.7 %copy-start.2 = (bf16[6144,192]{0,1:T(8,128)(2,1)S(1)}, bf16[6144,192]{0,1:T(8,128)(2,1)}, u32[]{:S(2)}) copy-start(bf16[6144,192]{0,1:T(8,128)(2,1)} %param.12) | copy-start | bytes 7077892
  33.0 3.8 %copy-start.5 = (s32[128,16]{0,1:T(8,128)S(1)}, s32[128,16]{0,1:T(8,128)}, u32[]{:S(2)}) copy-start(s32[128,16]{0,1:T(8,128)} %param.17) | copy-start | bytes 24580
  33.0 9.3 %copy-start.6 = (f32[16,2]{0,1:T(2,128)S(1)}, f32[16,2]{0,1:T(2,128)}, u32[]{:S(2)}) copy-start(f32[16,2]{0,1:T(2,128)} %param.16) | copy-start | bytes 388
  33.0 36.0 %all-to-all-start.1 = ((bf16[16,320,128]{2,1,0:T(8,128)(2,1)}), bf16[16,320,128]{2,1,0:T(8,128)(2,1)S(1)}, u32[]{:S(2)}, u32[]{:S(2)}) async-start(bf16[16,320,128]{2,1,0:T(8,128)(2,1)} %pack.1), calls=%async_computation.1 | async-start | bytes 2621440 | tf_op jit(solution)/shard_map/all_to_all | solution.py:523
  37.7 25.2 %collective-permute-start.2 = (bf16[256,384]{1,0:T(8,128)(2,1)}, bf16[256,384]{1,0:T(8,128)(2,1)}, u32[]{:S(2)}, u32[]{:S(2)}) collective-permute-start(bf16[256,384]{1,0:T(8,128)(2,1)} %pad_maximum_fusion), channel_id=1, source_target_pairs={{0,2},{1,3},{2,4},{3,5},{4,6},{5,7},{6,8},{7,9},{8,10},{9,11},{10,... | collective-permute-start | bytes 589832 | tf_op jit(solution)/shard_map/ppermute | solution.py:25
  44.7 13.0 %collective-permute-start.1 = (bf16[128,384]{1,0:T(8,128)(2,1)}, bf16[128,384]{1,0:T(8,128)(2,1)S(1)}, u32[]{:S(2)}, u32[]{:S(2)}) collective-permute-start(bf16[128,384]{1,0:T(8,128)(2,1)} %copy-done), channel_id=1, source_target_pairs={{0,4},{1,5},{2,6},{3,7},{4,8},{5,9},{6,10},{7,11},{8,12},{9,13},{1... | collective-permute-start | bytes 294920 | tf_op jit(solution)/shard_map/ppermute | solution.py:25
  62.8 0.9 %copy-start.1 = (bf16[128,384]{1,0:T(8,128)(2,1)S(1)}, bf16[128,384]{1,0:T(8,128)(2,1)}, u32[]{:S(2)}) copy-start(bf16[128,384]{1,0:T(8,128)(2,1)} %copy-done) | copy-start | bytes 294916
  68.0 1.0 %copy-start.3 = (f32[2048,128]{1,0:T(8,128)}, f32[2048,128]{1,0:T(8,128)S(1)}, u32[]{:S(2)}) copy-start(f32[2048,128]{1,0:T(8,128)S(1)} %window.1.win_ref) | copy-start | bytes 3145732
  69.0 7.8 %copy-start.4 = (f32[2048,128]{1,0:T(8,128)S(1)}, f32[2048,128]{1,0:T(8,128)}, u32[]{:S(2)}) copy-start(f32[2048,128]{1,0:T(8,128)} %copy-done.3) | copy-start | bytes 3145732
  69.0 7.7 %collective-permute-start.3 = (bf16[16,320,128]{2,1,0:T(8,128)(2,1)S(1)}, bf16[16,320,128]{2,1,0:T(8,128)(2,1)S(1)}, u32[]{:S(2)}, u32[]{:S(2)}) collective-permute-start(bf16[16,320,128]{2,1,0:T(8,128)(2,1)S(1)} %all-to-all-done.1.kv_ref), channel_id=1, source_target_pairs={{0,16},{16,0},{32,48},{48,32},{64,80},{80,64},{96,112},{112,96},{1... | collective-permute-start | bytes 3932168 | tf_op jit(solution)/shard_map/ppermute | solution.py:526

commit v4 on v1

--- a/solution.py
+++ b/solution.py
@@ -25,21 +25,31 @@
     return lax.ppermute(shard, axis, pairs)
 
 
-def pair_kernel(keys_ref, values_ref, out_ref):
-    out_ref[:, :192] = keys_ref[...].astype(jnp.float32).T.astype(out_ref.dtype)
+def pair_kernel(keys_hbm, values_hbm, out_ref, keys, sems):
+    loads = [
+        pltpu.make_async_copy(keys_hbm, keys, sems.at[0]),
+        pltpu.make_async_copy(values_hbm, out_ref.at[:, 256:], sems.at[1]),
+    ]
+    for load in loads:
+        load.start()
     out_ref[:, 192:256] = jnp.zeros((out_ref.shape[0], 64), out_ref.dtype)
-    out_ref[:, 256:] = values_ref[...]
+    loads[0].wait()
+    out_ref[:, :192] = keys[...].astype(jnp.float32).T.astype(out_ref.dtype)
+    loads[1].wait()
 
 
 def pair(keys, values):
+    keys = pltpu.with_memory_space_constraint(keys.T, pltpu.HBM)
+    values = pltpu.with_memory_space_constraint(values, pltpu.HBM)
     return pl.pallas_call(
         pair_kernel,
-        in_specs=[pl.BlockSpec(memory_space=pltpu.VMEM)] * 2,
+        in_specs=[pl.BlockSpec(memory_space=pltpu.HBM)] * 2,
         out_specs=pl.BlockSpec(memory_space=pltpu.VMEM),
-        out_shape=jax.ShapeDtypeStruct((keys.shape[0], 384), keys.dtype),
+        out_shape=jax.ShapeDtypeStruct((values.shape[0], 384), keys.dtype),
+        scratch_shapes=[pltpu.VMEM(keys.shape, keys.dtype), pltpu.SemaphoreType.DMA((2,))],
         compiler_params=pltpu.CompilerParams(vmem_limit_bytes=GRANT),
         name="pair",
-    )(keys.T, values)
+    )(keys, values)
 
 
 def silu(x):
@@ -329,41 +339,44 @@
     blocks = q_ref.shape[0] // sub
     plane = who[2]
 
-    def run(quarters):
+    def run(quarters, first, count):
+        def rows(j):
+            return pl.ds(pl.multiple_of((first + j) * sub, sub), sub)
+
         def score(j):
             return far_scores(
                 heads,
                 who[0],
                 core,
-                q_ref[j * sub : (j + 1) * sub],
+                q_ref[rows(j)],
                 kv_ref,
                 scratch[j % 2],
-                j * (sub // heads),
+                (first + j) * (sub // heads),
                 quarters,
             )
 
         tops = [score(0)]
-        for j in range(blocks):
-            if j + 1 < blocks:
+        for j in range(count):
+            if j + 1 < count:
                 tops.append(score(j + 1))
             mix = far_mix(scale, scratch[j % 2], tops[j], kv_ref, quarters)
-            finish(slice(j * sub, (j + 1) * sub), mix, tops[j])
-
-    @pl.when(plane < 4)
-    def _():
-        run(1)
-
-    @pl.when((plane >= 4) & (plane < 8))
-    def _():
-        run(2)
-
-    @pl.when(plane >= 8)
-    def _():
-        run(4)
+            finish(rows(j), first + j, mix, tops[j])
+
+    def run_parts(quarters):
+        half = blocks // 2
+
+        @pl.loop(0, 2)
+        def _(part):
+            run(quarters, part * half, half)
+
+    pl.when(plane < 4)(lambda: run(1, 0, blocks))
+    pl.when((plane >= 4) & (plane < 8))(lambda: run_parts(2))
+    pl.when((plane >= 8) & (plane < 12))(lambda: run_parts(3))
+    pl.when(plane >= 12)(lambda: run(4, 0, blocks))
 
 
 def first_kernel(scale, heads, who, q_ref, kv_ref, acc_ref, top_ref, *scratch):
-    def finish(here, accum, top):
+    def finish(here, j, accum, top):
         acc_ref[here] = accum
         top_ref[here] = jnp.broadcast_to(top, (accum.shape[0], 128))
 
@@ -389,10 +402,10 @@
     sub = even.shape[0]
 
     def move(j):
-        here = slice(j * sub, (j + 1) * sub)
+        here = pl.ds(pl.multiple_of(j * sub, sub), sub)
         return pltpu.make_async_copy(result.at[here], out_hbm.at[here], sems.at[j])
 
-    def finish(here, accum, top):
+    def finish(here, j, accum, top):
         other = top_ref[here]
         most = jnp.maximum(other, top)
         grow = jnp.exp2((other - most) * (scale * LOG2E))
@@ -402,7 +415,7 @@
         present = total > 0.0
         compressed = jnp.where(present, number / jnp.where(present, total, 1.0), 0.0)
         result[here] = (gate_ref[here, 0:1] * compressed + win_ref[here]).astype(result.dtype)
-        move(here.start // sub).start()
+        move(j).start()
 
     skewed(scale, heads, who, 1 - who[1], q_ref, kv_ref, (even, odd), finish)
     for j in range(q_ref.shape[0] // sub):

time: 85.9 us -> 85.1 us (level)
  local copies, waits for them, and re-layouts: 8.69 us -> 7.14 us
    unnamed x30 -> x26, local copies, waits for them, and re-layouts: 8.24 us -> 6.7 us
where the time goes in v4:
time: 85.1 us; the launch traced here: 83.7 us
  Pallas kernels  20.8 us (24%)
  blocking collectives  18.9 us (22%)
  waiting for transfers between devices  18.1 us (21%)
  starting transfers between devices  17.5 us (21%)
  local copies, waits for them, and re-layouts  7.14 us (8%)
  other arithmetic  0.92 us (1%)
    all_to_all x1, blocking collectives, local(): column = lax.all_to_all(payload, 'sa', 0, 0, axis_index_groups=groups)  18.9 us
    ppermute x3, waiting for transfers between devices, shifted(): return lax.ppermute(shard, axis, pairs)  18.1 us
    ppermute x3, starting transfers between devices, shifted(): return lax.ppermute(shard, axis, pairs)  11 us
    pallas_call x1, Pallas kernels, second_half(): pl.pallas_call(functools.partial(second_kernel, scale, heads), in_specs=[...  6.99 us
    unnamed x26, local copies, waits for them, and re-layouts  6.7 us
    pallas_call x1, Pallas kernels, first_half(): pl.pallas_call(functools.partial(first_kernel, scale, heads), in_specs=[p...  5.69 us
    all_to_all x1, starting transfers between devices, local(): mine = lax.all_to_all(copies, 'sb', 0, 0)  4.37 us
    pallas_call x1, Pallas kernels, window_branch(): pl.pallas_call(functools.partial(window_kernel, scale, heads), grid_spec=...  4.31 us
  transfers between devices with their start and end apart: 5, of which 3 were waited for; matrix products, arithmetic and copies ran while one was open for 4% of the time, Pallas kernels for 13%

profile of v4, /device:TPU:481, one launch (start us, length us, event | category | flops | bytes accessed | tf_op | source)
XLA Modules:
  0.0 83.7 jit_solution(10668664548371165837)
XLA Ops:
  0.0 0.9 %pair.1.pair_ref = bf16[128,384]{1,0:T(8,128)(2,1)S(1)} custom-call(bf16[192,128]{1,0:T(8,128)(2,1)} %bitcast.12, bf16[128,128]{1,0:T(8,128)(2,1)} %values_hbm.1), custom_call_target="tpu_custom_call" | custom-call | tf_op jit(solution)/shard_map/pair/pallas_call | solution.py:44
  0.9 3.2 %collective-permute-start = (bf16[128,384]{1,0:T(8,128)(2,1)S(1)}, bf16[128,384]{1,0:T(8,128)(2,1)S(1)}, u32[]{:S(2)}, u32[]{:S(2)}) collective-permute-start(bf16[128,384]{1,0:T(8,128)(2,1)S(1)} %pair.1.pair_ref), channel_id=1, source_target_pairs={{0,1},{1,2},{2,3},{3,4},{4,5},{5,6},{6,7},{7,8},{8,9},{9,10},{10,1... | collective-permute-start | bytes 294920 | tf_op jit(solution)/shard_map/ppermute | solution.py:25
  4.1 0.0 copy-start
  4.2 1.7 %copy-done = bf16[6144,192]{0,1:T(8,128)(2,1)S(1)} copy-done((bf16[6144,192]{0,1:T(8,128)(2,1)S(1)}, bf16[6144,192]{0,1:T(8,128)(2,1)}, u32[]{:S(2)}) %copy-start) | copy-done | bytes 2359320
  5.8 0.0 copy-start.2
  5.8 1.2 %copy-done.2 = bf16[4096,128]{1,0:T(8,128)(2,1)S(1)} copy-done((bf16[4096,128]{1,0:T(8,128)(2,1)S(1)}, bf16[4096,128]{1,0:T(8,128)(2,1)}, u32[]{:S(2)}) %copy-start.2) | copy-done | bytes 1048600
  7.0 0.0 copy-start.1
  7.0 0.0 copy-start.3
  7.0 0.0 copy-start.6
  7.0 0.0 copy-start.7
  7.0 0.9 %own_blocks.1.hidden_ref = f32[8,384]{1,0:T(8,128)S(1)} custom-call(bf16[128,384]{1,0:T(8,128)(2,1)S(1)} %pair.1.pair_ref, bf16[192,6144]{1,0:T(8,128)(2,1)S(1)} %bitcast.7, bf16[4096,128]{1,0:T(8,128)(2,1)S(1)} %copy-done.2), custom_call_target="tpu_custom_call" | custom-call | flops 1000000000 | bytes 8000000 | tf_op jit(solution)/shard_map/own_blocks/pallas_call | solution.py:102
  7.9 3.7 %collective-permute-done.before_ref.one_ref = bf16[128,384]{1,0:T(8,128)(2,1)S(1)} collective-permute-done((bf16[128,384]{1,0:T(8,128)(2,1)S(1)}, bf16[128,384]{1,0:T(8,128)(2,1)S(1)}, u32[]{:S(2)}, u32[]{:S(2)}) %collective-permute-start) | collective-permute-done | bytes 98336 | tf_op jit(solution)/shard_map/ppermute | solution.py:25
  11.7 0.0 copy-done.1
  11.7 0.0 copy-done.3
  11.7 0.0 copy-done.6
  11.7 0.0 copy-done.7
  11.7 0.0 copy-start.4
  11.7 0.7 summary.1
  12.4 18.9 %all_to_all.10.column_ref = bf16[16,24,128]{2,1,0:T(8,128)(2,1)S(1)} all-to-all(bf16[16,24,128]{2,1,0:T(8,128)(2,1)S(1)} %summary.1), channel_id=1, replica_groups={{0,32,64,96,128,160,192,224,256,288,320,352,384,416,448,480},{16,48,80,..., dimensions={0} | all-to-all | bytes 196608 | tf_op jit(solution)/shard_map/all_to_all | solution.py:486
  31.3 1.3 %pack.1 = bf16[16,320,128]{2,1,0:T(8,128)(2,1)} custom-call(bf16[16,24,128]{2,1,0:T(8,128)(2,1)S(1)} %all_to_all.10.column_ref), custom_call_target="tpu_custom_call" | custom-call | tf_op jit(solution)/shard_map/pack/pallas_call | solution.py:190
  32.6 0.0 copy-start.10
  32.6 0.0 copy-start.11
  32.6 4.4 %all-to-all-start.1 = ((bf16[16,320,128]{2,1,0:T(8,128)(2,1)}), bf16[16,320,128]{2,1,0:T(8,128)(2,1)S(1)}, u32[]{:S(2)}, u32[]{:S(2)}) async-start(bf16[16,320,128]{2,1,0:T(8,128)(2,1)} %pack.1), calls=%async_computation.1 | async-start | bytes 2621440 | tf_op jit(solution)/shard_map/all_to_all | solution.py:496
  37.0 0.0 copy-done.10
  37.0 0.1 copy.16
  37.1 0.1 eq.21
  37.3 0.0 copy-done.4
  37.3 0.7 pad_maximum_fusion
  38.0 4.7 %collective-permute-start.2 = (bf16[256,384]{1,0:T(8,128)(2,1)}, bf16[256,384]{1,0:T(8,128)(2,1)}, u32[]{:S(2)}, u32[]{:S(2)}) collective-permute-start(bf16[256,384]{1,0:T(8,128)(2,1)} %pad_maximum_fusion), channel_id=1, source_target_pairs={{0,2},{1,3},{2,4},{3,5},{4,6},{5,7},{6,8},{7,9},{8,10},{9,11},{10,... | collective-permute-start | bytes 589832 | tf_op jit(solution)/shard_map/ppermute | solution.py:25
  42.7 0.0 copy-done.11
  42.7 0.1 multiply_reduce_fusion
  42.9 0.4 copy.17.gate_ref
  43.2 1.8 %copy.15 = bf16[128,16,192]{2,1,0:T(8,128)(2,1)S(1)} copy(bf16[128,16,192]{0,2,1:T(8,128)(2,1)} %param.9) | data formatting | bytes 1572864 | tf_op args[0]
  45.1 3.1 %collective-permute-start.1 = (bf16[128,384]{1,0:T(8,128)(2,1)S(1)}, bf16[128,384]{1,0:T(8,128)(2,1)S(1)}, u32[]{:S(2)}, u32[]{:S(2)}) collective-permute-start(bf16[128,384]{1,0:T(8,128)(2,1)S(1)} %pair.1.pair_ref), channel_id=1, source_target_pairs={{0,4},{1,5},{2,6},{3,7},{4,8},{5,9},{6,10},{7,11},{8,12},{9,13},{1... | collective-permute-start | bytes 294920 | tf_op jit(solution)/shard_map/ppermute | solution.py:25
  48.2 0.1 pad_add_fusion.who
  48.2 9.3 %collective-permute-done.1.four_ref = bf16[128,384]{1,0:T(8,128)(2,1)S(1)} collective-permute-done((bf16[128,384]{1,0:T(8,128)(2,1)S(1)}, bf16[128,384]{1,0:T(8,128)(2,1)S(1)}, u32[]{:S(2)}, u32[]{:S(2)}) %collective-permute-start.1) | collective-permute-done | bytes 98336 | tf_op jit(solution)/shard_map/ppermute | solution.py:25
  57.5 5.0 %collective-permute-done.2.two_ref = bf16[256,384]{1,0:T(8,128)(2,1)} collective-permute-done((bf16[256,384]{1,0:T(8,128)(2,1)}, bf16[256,384]{1,0:T(8,128)(2,1)}, u32[]{:S(2)}, u32[]{:S(2)}) %collective-permute-start.2) | collective-permute-done | bytes 196640 | tf_op jit(solution)/shard_map/ppermute | solution.py:25
  62.6 0.0 copy-start.5
  62.6 0.9 %copy-done.5 = bf16[128,384]{1,0:T(8,128)(2,1)S(1)} copy-done((bf16[128,384]{1,0:T(8,128)(2,1)S(1)}, bf16[128,384]{1,0:T(8,128)(2,1)}, u32[]{:S(2)}) %copy-start.5) | copy-done | bytes 98328
  63.5 4.3 %window.1.win_ref = f32[2048,128]{1,0:T(8,128)S(1)} custom-call(s32[3]{0:T(128)S(1)} %pad_add_fusion.who, bf16[2048,192]{1,0:T(8,128)(2,1)S(1)} %bitcast.9, bf16[128,384]{1,0:T(8,128)(2,1)S(1)} %collective-permute-done.1.four_ref, bf16[256,384]{1,0:T(8,128)(2,1)} %collective-permute-done.2.two_ref, bf16[128,384]{1,0:T(8,128)(2,1)S(1)} %copy-done.5, ...), custom_call_target="tpu_custom_call" | custom-call | flops 1342177280 | bytes 4000000 | tf_op jit(solution)/shard_map/window/pallas_call | solution.py:267
  67.8 0.0 copy-start.8
  67.8 1.0 %copy-done.8 = f32[2048,128]{1,0:T(8,128)} copy-done((f32[2048,128]{1,0:T(8,128)}, f32[2048,128]{1,0:T(8,128)S(1)}, u32[]{:S(2)}) %copy-start.8) | copy-done | bytes 1048600
  68.8 0.0 all-to-all-done.1.kv_ref
  68.8 2.0 %collective-permute-start.3 = (bf16[16,320,128]{2,1,0:T(8,128)(2,1)S(1)}, bf16[16,320,128]{2,1,0:T(8,128)(2,1)S(1)}, u32[]{:S(2)}, u32[]{:S(2)}) collective-permute-start(bf16[16,320,128]{2,1,0:T(8,128)(2,1)S(1)} %all-to-all-done.1.kv_ref), channel_id=1, source_target_pairs={{0,16},{16,0},{32,48},{48,32},{64,80},{80,64},{96,112},{112,96},{1... | collective-permute-start | bytes 3932168 | tf_op jit(solution)/shard_map/ppermute | solution.py:499
  70.8 5.7 %first_half.1 = (f32[2048,256]{1,0:T(8,128)S(1)}, f32[2048,128]{1,0:T(8,128)S(1)}) custom-call(s32[3]{0:T(128)S(1)} %pad_add_fusion.who, bf16[2048,192]{1,0:T(8,128)(2,1)S(1)} %bitcast.10, bf16[16,320,128]{2,1,0:T(8,128)(2,1)S(1)} %all-to-all-done.1.kv_ref), custom_call_target="tpu_custom_call" | custom-call | flops 4294967296 | bytes 3000000 | tf_op jit(solution)/shard_map/first_half/pallas_call | solution.py:429
  76.5 0.0 collective-permute-done.3.kv_ref
  76.5 0.0 copy-done.9
  76.5 7.0 %second_half.1 = bf16[2048,128]{1,0:T(8,128)(2,1)} custom-call(s32[3]{0:T(128)S(1)} %pad_add_fusion.who, bf16[2048,192]{1,0:T(8,128)(2,1)S(1)} %bitcast.11, bf16[16,320,128]{2,1,0:T(8,128)(2,1)S(1)} %collective-permute-done.3.kv_ref, f32[2048,256]{1,0:T(8,128)S(1)} %get-tuple-element.16.acc_ref, f32[2048,128]{1,0:T(8,128)S(1)} %get-tuple-element.17.top_ref, ...), custom_call_target="tpu_custom_call" | custom-call | flops 4294967296 | bytes 5000000 | tf_op jit(solution)/shard_map/second_half/pallas_call | solution.py:450
  (2 shorter events, 0.0 us)
Async XLA Ops:
  0.9 10.7 %collective-permute-start = (bf16[128,384]{1,0:T(8,128)(2,1)S(1)}, bf16[128,384]{1,0:T(8,128)(2,1)S(1)}, u32[]{:S(2)}, u32[]{:S(2)}) collective-permute-start(bf16[128,384]{1,0:T(8,128)(2,1)S(1)} %pair.1.pair_ref), channel_id=1, source_target_pairs={{0,1},{1,2},{2,3},{3,4},{4,5},{5,6},{6,7},{7,8},{8,9},{9,10},{10,1... | collective-permute-start | bytes 294920 | tf_op jit(solution)/shard_map/ppermute | solution.py:25
  4.1 1.7 %copy-start = (bf16[6144,192]{0,1:T(8,128)(2,1)S(1)}, bf16[6144,192]{0,1:T(8,128)(2,1)}, u32[]{:S(2)}) copy-start(bf16[6144,192]{0,1:T(8,128)(2,1)} %param.12) | copy-start | bytes 7077892
  5.8 1.2 %copy-start.2 = (bf16[4096,128]{1,0:T(8,128)(2,1)S(1)}, bf16[4096,128]{1,0:T(8,128)(2,1)}, u32[]{:S(2)}) copy-start(bf16[4096,128]{1,0:T(8,128)(2,1)} %vfirst_ref.3) | copy-start | bytes 3145732
  7.0 4.6 %copy-start.1 = (bf16[6144,192]{0,1:T(8,128)(2,1)S(1)}, bf16[6144,192]{0,1:T(8,128)(2,1)}, u32[]{:S(2)}) copy-start(bf16[6144,192]{0,1:T(8,128)(2,1)} %param.12) | copy-start | bytes 7077892
  7.0 4.6 %copy-start.3 = (bf16[4096,128]{1,0:T(8,128)(2,1)S(1)}, bf16[4096,128]{1,0:T(8,128)(2,1)}, u32[]{:S(2)}) copy-start(bf16[4096,128]{1,0:T(8,128)(2,1)} %vfirst_ref.3) | copy-start | bytes 3145732
  7.0 4.6 %copy-start.6 = (bf16[192,192]{1,0:T(8,128)(2,1)S(1)}, bf16[192,192]{1,0:T(8,128)(2,1)}, u32[]{:S(2)}) copy-start(bf16[192,192]{1,0:T(8,128)(2,1)} %ksecond_ref.1) | copy-start | bytes 221188
  7.0 4.6 %copy-start.7 = (bf16[128,128]{1,0:T(8,128)(2,1)S(1)}, bf16[128,128]{1,0:T(8,128)(2,1)}, u32[]{:S(2)}) copy-start(bf16[128,128]{1,0:T(8,128)(2,1)} %vsecond_ref.1) | copy-start | bytes 98308
  11.7 25.6 %copy-start.4 = (bf16[128,384]{1,0:T(8,128)(2,1)}, bf16[128,384]{1,0:T(8,128)(2,1)S(1)}, u32[]{:S(2)}) copy-start(bf16[128,384]{1,0:T(8,128)(2,1)S(1)} %collective-permute-done.before_ref.one_ref) | copy-start | bytes 294916
  32.6 4.4 %copy-start.10 = (s32[128,16]{0,1:T(8,128)S(1)}, s32[128,16]{0,1:T(8,128)}, u32[]{:S(2)}) copy-start(s32[128,16]{0,1:T(8,128)} %param.17) | copy-start | bytes 24580
  32.6 10.1 %copy-start.11 = (f32[16,2]{0,1:T(2,128)S(1)}, f32[16,2]{0,1:T(2,128)}, u32[]{:S(2)}) copy-start(f32[16,2]{0,1:T(2,128)} %param.16) | copy-start | bytes 388
  32.6 36.1 %all-to-all-start.1 = ((bf16[16,320,128]{2,1,0:T(8,128)(2,1)}), bf16[16,320,128]{2,1,0:T(8,128)(2,1)S(1)}, u32[]{:S(2)}, u32[]{:S(2)}) async-start(bf16[16,320,128]{2,1,0:T(8,128)(2,1)} %pack.1), calls=%async_computation.1 | async-start | bytes 2621440 | tf_op jit(solution)/shard_map/all_to_all | solution.py:496
  38.0 24.6 %collective-permute-start.2 = (bf16[256,384]{1,0:T(8,128)(2,1)}, bf16[256,384]{1,0:T(8,128)(2,1)}, u32[]{:S(2)}, u32[]{:S(2)}) collective-permute-start(bf16[256,384]{1,0:T(8,128)(2,1)} %pad_maximum_fusion), channel_id=1, source_target_pairs={{0,2},{1,3},{2,4},{3,5},{4,6},{5,7},{6,8},{7,9},{8,10},{9,11},{10,... | collective-permute-start | bytes 589832 | tf_op jit(solution)/shard_map/ppermute | solution.py:25
  45.1 12.5 %collective-permute-start.1 = (bf16[128,384]{1,0:T(8,128)(2,1)S(1)}, bf16[128,384]{1,0:T(8,128)(2,1)S(1)}, u32[]{:S(2)}, u32[]{:S(2)}) collective-permute-start(bf16[128,384]{1,0:T(8,128)(2,1)S(1)} %pair.1.pair_ref), channel_id=1, source_target_pairs={{0,4},{1,5},{2,6},{3,7},{4,8},{5,9},{6,10},{7,11},{8,12},{9,13},{1... | collective-permute-start | bytes 294920 | tf_op jit(solution)/shard_map/ppermute | solution.py:25
  62.6 0.9 %copy-start.5 = (bf16[128,384]{1,0:T(8,128)(2,1)S(1)}, bf16[128,384]{1,0:T(8,128)(2,1)}, u32[]{:S(2)}) copy-start(bf16[128,384]{1,0:T(8,128)(2,1)} %copy-done.4) | copy-start | bytes 294916
  67.8 1.0 %copy-start.8 = (f32[2048,128]{1,0:T(8,128)}, f32[2048,128]{1,0:T(8,128)S(1)}, u32[]{:S(2)}) copy-start(f32[2048,128]{1,0:T(8,128)S(1)} %window.1.win_ref) | copy-start | bytes 3145732
  68.8 7.8 %copy-start.9 = (f32[2048,128]{1,0:T(8,128)S(1)}, f32[2048,128]{1,0:T(8,128)}, u32[]{:S(2)}) copy-start(f32[2048,128]{1,0:T(8,128)} %copy-done.8) | copy-start | bytes 3145732
  68.8 7.7 %collective-permute-start.3 = (bf16[16,320,128]{2,1,0:T(8,128)(2,1)S(1)}, bf16[16,320,128]{2,1,0:T(8,128)(2,1)S(1)}, u32[]{:S(2)}, u32[]{:S(2)}) collective-permute-start(bf16[16,320,128]{2,1,0:T(8,128)(2,1)S(1)} %all-to-all-done.1.kv_ref), channel_id=1, source_target_pairs={{0,16},{16,0},{32,48},{48,32},{64,80},{80,64},{96,112},{112,96},{1... | collective-permute-start | bytes 3932168 | tf_op jit(solution)/shard_map/ppermute | solution.py:499

commit v5 on v4

--- a/solution.py
+++ b/solution.py
@@ -289,7 +289,7 @@
     )(who, q, four, two, one, paired, gates)
 
 
-def far_scores(heads, device, core, q, kv_ref, s_ref, base, quarters):
+def far_scores(heads, device, core, q, kv_ref, s_ref, base, tiles):
     block = q.shape[0]
     zeros = jnp.zeros((block, 64), q.dtype)
     queries = (
@@ -299,38 +299,31 @@
     token = base + lax.broadcasted_iota(jnp.int32, (block, 256), 0) // heads
     lane = lax.broadcasted_iota(jnp.int32, (1, 256), 1)
     top = None
-    for quarter in range(quarters):
-        for g in range(kv_ref.shape[0] // 8):
-            some = slice(8 * g, 8 * g + 8)
-            begin = 32 * quarter
-            low = kv_ref[some, begin : begin + 32].reshape(256, 128)
-            begin = 128 + 32 * (quarter % 2)
-            high = kv_ref[some, begin : begin + 32].reshape(256, 128)
-            s = nt(queries[quarter // 2], jnp.concatenate([low, high], axis=1))
-            z = 4 * quarter + (lane % 32) // 8
-            owner = (2 * z + core) * 16 + 8 * g + lane // 32
-            end = (owner - device) * 128 + STRIDE * (lane % 8) + STRIDE - 1
-            s = jnp.where(end <= token, s, LOW)
-            slot = 2 * quarter + g
-            s_ref[:, 256 * slot : 256 * slot + 256] = s
-            most = jnp.maximum(s[:, :128], s[:, 128:])
-            top = most if top is None else jnp.maximum(top, most)
+    for tile in range(tiles):
+        begin = 16 * tile
+        low = kv_ref[:, begin : begin + 16].reshape(256, 128)
+        begin = 128 + 16 * (tile % 4)
+        high = kv_ref[:, begin : begin + 16].reshape(256, 128)
+        s = nt(queries[tile // 4], jnp.concatenate([low, high], axis=1))
+        z = 2 * tile + (lane % 16) // 8
+        owner = (2 * z + core) * 16 + lane // 16
+        end = (owner - device) * 128 + STRIDE * (lane % 8) + STRIDE - 1
+        s = jnp.where(end <= token, s, LOW)
+        s_ref[:, 256 * tile : 256 * tile + 256] = s
+        most = jnp.maximum(s[:, :128], s[:, 128:])
+        top = most if top is None else jnp.maximum(top, most)
     return jnp.maximum(jnp.max(top, axis=1, keepdims=True), FLOOR)
 
 
-def far_mix(scale, s_ref, top, kv_ref, quarters):
+def far_mix(scale, s_ref, top, kv_ref, tiles):
     ones = jnp.ones((256, 128), jnp.bfloat16)
     accum = jnp.zeros((s_ref.shape[0], 256), jnp.float32)
-    for quarter in range(quarters):
-        for g in range(kv_ref.shape[0] // 8):
-            slot = 2 * quarter + g
-            s = s_ref[:, 256 * slot : 256 * slot + 256]
-            p = jnp.exp2((s - top) * (scale * LOG2E)).astype(jnp.bfloat16)
-            begin = 192 + 32 * quarter
-            v = kv_ref[8 * g : 8 * g + 8, begin : begin + 32].reshape(256, 128)
-            accum += jnp.dot(
-                p, jnp.concatenate([v, ones], axis=1), preferred_element_type=jnp.float32
-            )
+    for tile in range(tiles):
+        s = s_ref[:, 256 * tile : 256 * tile + 256]
+        p = jnp.exp2((s - top) * (scale * LOG2E)).astype(jnp.bfloat16)
+        begin = 192 + 16 * tile
+        v = kv_ref[:, begin : begin + 16].reshape(256, 128)
+        accum += jnp.dot(p, jnp.concatenate([v, ones], axis=1), preferred_element_type=jnp.float32)
     return accum
 
 
@@ -339,7 +332,7 @@
     blocks = q_ref.shape[0] // sub
     plane = who[2]
 
-    def run(quarters, first, count):
+    def run(tiles, first, count):
         def rows(j):
             return pl.ds(pl.multiple_of((first + j) * sub, sub), sub)
 
@@ -352,27 +345,38 @@
                 kv_ref,
                 scratch[j % 2],
                 (first + j) * (sub // heads),
-                quarters,
+                tiles,
             )
 
         tops = [score(0)]
         for j in range(count):
             if j + 1 < count:
                 tops.append(score(j + 1))
-            mix = far_mix(scale, scratch[j % 2], tops[j], kv_ref, quarters)
+            mix = far_mix(scale, scratch[j % 2], tops[j], kv_ref, tiles)
             finish(rows(j), first + j, mix, tops[j])
 
-    def run_parts(quarters):
+    def run_parts(tiles):
         half = blocks // 2
 
         @pl.loop(0, 2)
         def _(part):
-            run(quarters, part * half, half)
-
-    pl.when(plane < 4)(lambda: run(1, 0, blocks))
-    pl.when((plane >= 4) & (plane < 8))(lambda: run_parts(2))
-    pl.when((plane >= 8) & (plane < 12))(lambda: run_parts(3))
-    pl.when(plane >= 12)(lambda: run(4, 0, blocks))
+            run(tiles, part * half, half)
+
+    begin = 0
+    for until, tiles, whole in (
+        (2, 1, True),
+        (4, 2, False),
+        (6, 3, True),
+        (8, 4, False),
+        (12, 6, False),
+        (16, 8, True),
+    ):
+        here = (plane >= begin) & (plane < until)
+        if whole:
+            pl.when(here)(functools.partial(run, tiles, 0, blocks))
+        else:
+            pl.when(here)(functools.partial(run_parts, tiles))
+        begin = until
 
 
 def first_kernel(scale, heads, who, q_ref, kv_ref, acc_ref, top_ref, *scratch):

time: 85.1 us -> 85.2 us (level)
  no operation moved by 1% of the time
where the time goes in v5:
time: 85.2 us; the launch traced here: 83.8 us
  Pallas kernels  20.8 us (24%)
  blocking collectives  18.9 us (22%)
  waiting for transfers between devices  18.1 us (21%)
  starting transfers between devices  17.5 us (21%)
  local copies, waits for them, and re-layouts  7.14 us (8%)
  other arithmetic  0.92 us (1%)
    all_to_all x1, blocking collectives, local(): column = lax.all_to_all(payload, 'sa', 0, 0, axis_index_groups=groups)  18.9 us
    ppermute x3, waiting for transfers between devices, shifted(): return lax.ppermute(shard, axis, pairs)  18.1 us
    ppermute x3, starting transfers between devices, shifted(): return lax.ppermute(shard, axis, pairs)  11 us
    pallas_call x1, Pallas kernels, second_half(): pl.pallas_call(functools.partial(second_kernel, scale, heads), in_specs=[...  7.01 us
    unnamed x26, local copies, waits for them, and re-layouts  6.7 us
    pallas_call x1, Pallas kernels, first_half(): pl.pallas_call(functools.partial(first_kernel, scale, heads), in_specs=[p...  5.72 us
    all_to_all x1, starting transfers between devices, local(): mine = lax.all_to_all(copies, 'sb', 0, 0)  4.37 us
    pallas_call x1, Pallas kernels, window_branch(): pl.pallas_call(functools.partial(window_kernel, scale, heads), grid_spec=...  4.31 us
  transfers between devices with their start and end apart: 5, of which 3 were waited for; matrix products, arithmetic and copies ran while one was open for 4% of the time, Pallas kernels for 13%

profile of v5, /device:TPU:481, one launch (start us, length us, event | category | flops | bytes accessed | tf_op | source)
XLA Modules:
  0.0 83.8 jit_solution(11884946066014044914)
XLA Ops:
  0.0 0.9 %pair.1.pair_ref = bf16[128,384]{1,0:T(8,128)(2,1)S(1)} custom-call(bf16[192,128]{1,0:T(8,128)(2,1)} %bitcast.12, bf16[128,128]{1,0:T(8,128)(2,1)} %values_hbm.1), custom_call_target="tpu_custom_call" | custom-call | tf_op jit(solution)/shard_map/pair/pallas_call | solution.py:44
  0.9 3.2 %collective-permute-start = (bf16[128,384]{1,0:T(8,128)(2,1)S(1)}, bf16[128,384]{1,0:T(8,128)(2,1)S(1)}, u32[]{:S(2)}, u32[]{:S(2)}) collective-permute-start(bf16[128,384]{1,0:T(8,128)(2,1)S(1)} %pair.1.pair_ref), channel_id=1, source_target_pairs={{0,1},{1,2},{2,3},{3,4},{4,5},{5,6},{6,7},{7,8},{8,9},{9,10},{10,1... | collective-permute-start | bytes 294920 | tf_op jit(solution)/shard_map/ppermute | solution.py:25
  4.1 0.0 copy-start
  4.2 1.7 %copy-done = bf16[6144,192]{0,1:T(8,128)(2,1)S(1)} copy-done((bf16[6144,192]{0,1:T(8,128)(2,1)S(1)}, bf16[6144,192]{0,1:T(8,128)(2,1)}, u32[]{:S(2)}) %copy-start) | copy-done | bytes 2359320
  5.8 0.0 copy-start.2
  5.8 1.2 %copy-done.2 = bf16[4096,128]{1,0:T(8,128)(2,1)S(1)} copy-done((bf16[4096,128]{1,0:T(8,128)(2,1)S(1)}, bf16[4096,128]{1,0:T(8,128)(2,1)}, u32[]{:S(2)}) %copy-start.2) | copy-done | bytes 1048600
  7.0 0.0 copy-start.1
  7.0 0.0 copy-start.3
  7.0 0.0 copy-start.6
  7.0 0.0 copy-start.7
  7.0 0.9 %own_blocks.1.hidden_ref = f32[8,384]{1,0:T(8,128)S(1)} custom-call(bf16[128,384]{1,0:T(8,128)(2,1)S(1)} %pair.1.pair_ref, bf16[192,6144]{1,0:T(8,128)(2,1)S(1)} %bitcast.7, bf16[4096,128]{1,0:T(8,128)(2,1)S(1)} %copy-done.2), custom_call_target="tpu_custom_call" | custom-call | flops 1000000000 | bytes 8000000 | tf_op jit(solution)/shard_map/own_blocks/pallas_call | solution.py:102
  7.9 3.7 %collective-permute-done.before_ref.one_ref = bf16[128,384]{1,0:T(8,128)(2,1)S(1)} collective-permute-done((bf16[128,384]{1,0:T(8,128)(2,1)S(1)}, bf16[128,384]{1,0:T(8,128)(2,1)S(1)}, u32[]{:S(2)}, u32[]{:S(2)}) %collective-permute-start) | collective-permute-done | bytes 98336 | tf_op jit(solution)/shard_map/ppermute | solution.py:25
  11.7 0.0 copy-done.1
  11.7 0.0 copy-done.3
  11.7 0.0 copy-done.6
  11.7 0.0 copy-done.7
  11.7 0.0 copy-start.4
  11.7 0.7 summary.1
  12.4 18.9 %all_to_all.10.column_ref = bf16[16,24,128]{2,1,0:T(8,128)(2,1)S(1)} all-to-all(bf16[16,24,128]{2,1,0:T(8,128)(2,1)S(1)} %summary.1), channel_id=1, replica_groups={{0,32,64,96,128,160,192,224,256,288,320,352,384,416,448,480},{16,48,80,..., dimensions={0} | all-to-all | bytes 196608 | tf_op jit(solution)/shard_map/all_to_all | solution.py:490
  31.3 1.3 %pack.1 = bf16[16,320,128]{2,1,0:T(8,128)(2,1)} custom-call(bf16[16,24,128]{2,1,0:T(8,128)(2,1)S(1)} %all_to_all.10.column_ref), custom_call_target="tpu_custom_call" | custom-call | tf_op jit(solution)/shard_map/pack/pallas_call | solution.py:190
  32.6 0.0 copy-start.10
  32.6 0.0 copy-start.11
  32.6 4.4 %all-to-all-start.1 = ((bf16[16,320,128]{2,1,0:T(8,128)(2,1)}), bf16[16,320,128]{2,1,0:T(8,128)(2,1)S(1)}, u32[]{:S(2)}, u32[]{:S(2)}) async-start(bf16[16,320,128]{2,1,0:T(8,128)(2,1)} %pack.1), calls=%async_computation.1 | async-start | bytes 2621440 | tf_op jit(solution)/shard_map/all_to_all | solution.py:500
  37.0 0.0 copy-done.10
  37.0 0.1 copy.16
  37.1 0.1 eq.21
  37.3 0.0 copy-done.4
  37.3 0.7 pad_maximum_fusion
  38.0 4.7 %collective-permute-start.2 = (bf16[256,384]{1,0:T(8,128)(2,1)}, bf16[256,384]{1,0:T(8,128)(2,1)}, u32[]{:S(2)}, u32[]{:S(2)}) collective-permute-start(bf16[256,384]{1,0:T(8,128)(2,1)} %pad_maximum_fusion), channel_id=1, source_target_pairs={{0,2},{1,3},{2,4},{3,5},{4,6},{5,7},{6,8},{7,9},{8,10},{9,11},{10,... | collective-permute-start | bytes 589832 | tf_op jit(solution)/shard_map/ppermute | solution.py:25
  42.7 0.0 copy-done.11
  42.7 0.1 multiply_reduce_fusion
  42.9 0.4 copy.17.gate_ref
  43.2 1.8 %copy.15 = bf16[128,16,192]{2,1,0:T(8,128)(2,1)S(1)} copy(bf16[128,16,192]{0,2,1:T(8,128)(2,1)} %param.9) | data formatting | bytes 1572864 | tf_op args[0]
  45.1 3.1 %collective-permute-start.1 = (bf16[128,384]{1,0:T(8,128)(2,1)S(1)}, bf16[128,384]{1,0:T(8,128)(2,1)S(1)}, u32[]{:S(2)}, u32[]{:S(2)}) collective-permute-start(bf16[128,384]{1,0:T(8,128)(2,1)S(1)} %pair.1.pair_ref), channel_id=1, source_target_pairs={{0,4},{1,5},{2,6},{3,7},{4,8},{5,9},{6,10},{7,11},{8,12},{9,13},{1... | collective-permute-start | bytes 294920 | tf_op jit(solution)/shard_map/ppermute | solution.py:25
  48.2 0.1 pad_add_fusion.who
  48.2 9.3 %collective-permute-done.1.four_ref = bf16[128,384]{1,0:T(8,128)(2,1)S(1)} collective-permute-done((bf16[128,384]{1,0:T(8,128)(2,1)S(1)}, bf16[128,384]{1,0:T(8,128)(2,1)S(1)}, u32[]{:S(2)}, u32[]{:S(2)}) %collective-permute-start.1) | collective-permute-done | bytes 98336 | tf_op jit(solution)/shard_map/ppermute | solution.py:25
  57.5 5.0 %collective-permute-done.2.two_ref = bf16[256,384]{1,0:T(8,128)(2,1)} collective-permute-done((bf16[256,384]{1,0:T(8,128)(2,1)}, bf16[256,384]{1,0:T(8,128)(2,1)}, u32[]{:S(2)}, u32[]{:S(2)}) %collective-permute-start.2) | collective-permute-done | bytes 196640 | tf_op jit(solution)/shard_map/ppermute | solution.py:25
  62.6 0.0 copy-start.5
  62.6 0.9 %copy-done.5 = bf16[128,384]{1,0:T(8,128)(2,1)S(1)} copy-done((bf16[128,384]{1,0:T(8,128)(2,1)S(1)}, bf16[128,384]{1,0:T(8,128)(2,1)}, u32[]{:S(2)}) %copy-start.5) | copy-done | bytes 98328
  63.5 4.3 %window.1.win_ref = f32[2048,128]{1,0:T(8,128)S(1)} custom-call(s32[3]{0:T(128)S(1)} %pad_add_fusion.who, bf16[2048,192]{1,0:T(8,128)(2,1)S(1)} %bitcast.9, bf16[128,384]{1,0:T(8,128)(2,1)S(1)} %collective-permute-done.1.four_ref, bf16[256,384]{1,0:T(8,128)(2,1)} %collective-permute-done.2.two_ref, bf16[128,384]{1,0:T(8,128)(2,1)S(1)} %copy-done.5, ...), custom_call_target="tpu_custom_call" | custom-call | flops 1342177280 | bytes 4000000 | tf_op jit(solution)/shard_map/window/pallas_call | solution.py:267
  67.8 0.0 copy-start.8
  67.8 1.0 %copy-done.8 = f32[2048,128]{1,0:T(8,128)} copy-done((f32[2048,128]{1,0:T(8,128)}, f32[2048,128]{1,0:T(8,128)S(1)}, u32[]{:S(2)}) %copy-start.8) | copy-done | bytes 1048600
  68.8 0.0 all-to-all-done.1.kv_ref
  68.8 2.0 %collective-permute-start.3 = (bf16[16,320,128]{2,1,0:T(8,128)(2,1)S(1)}, bf16[16,320,128]{2,1,0:T(8,128)(2,1)S(1)}, u32[]{:S(2)}, u32[]{:S(2)}) collective-permute-start(bf16[16,320,128]{2,1,0:T(8,128)(2,1)S(1)} %all-to-all-done.1.kv_ref), channel_id=1, source_target_pairs={{0,16},{16,0},{32,48},{48,32},{64,80},{80,64},{96,112},{112,96},{1... | collective-permute-start | bytes 3932168 | tf_op jit(solution)/shard_map/ppermute | solution.py:503
  70.8 5.7 %first_half.1 = (f32[2048,256]{1,0:T(8,128)S(1)}, f32[2048,128]{1,0:T(8,128)S(1)}) custom-call(s32[3]{0:T(128)S(1)} %pad_add_fusion.who, bf16[2048,192]{1,0:T(8,128)(2,1)S(1)} %bitcast.10, bf16[16,320,128]{2,1,0:T(8,128)(2,1)S(1)} %all-to-all-done.1.kv_ref), custom_call_target="tpu_custom_call" | custom-call | flops 4294967296 | bytes 3000000 | tf_op jit(solution)/shard_map/first_half/pallas_call | solution.py:433
  76.5 0.0 collective-permute-done.3.kv_ref
  76.5 0.0 copy-done.9
  76.6 7.0 %second_half.1 = bf16[2048,128]{1,0:T(8,128)(2,1)} custom-call(s32[3]{0:T(128)S(1)} %pad_add_fusion.who, bf16[2048,192]{1,0:T(8,128)(2,1)S(1)} %bitcast.11, bf16[16,320,128]{2,1,0:T(8,128)(2,1)S(1)} %collective-permute-done.3.kv_ref, f32[2048,256]{1,0:T(8,128)S(1)} %get-tuple-element.16.acc_ref, f32[2048,128]{1,0:T(8,128)S(1)} %get-tuple-element.17.top_ref, ...), custom_call_target="tpu_custom_call" | custom-call | flops 4294967296 | bytes 5000000 | tf_op jit(solution)/shard_map/second_half/pallas_call | solution.py:454
  (2 shorter events, 0.0 us)
Async XLA Ops:
  0.9 10.7 %collective-permute-start = (bf16[128,384]{1,0:T(8,128)(2,1)S(1)}, bf16[128,384]{1,0:T(8,128)(2,1)S(1)}, u32[]{:S(2)}, u32[]{:S(2)}) collective-permute-start(bf16[128,384]{1,0:T(8,128)(2,1)S(1)} %pair.1.pair_ref), channel_id=1, source_target_pairs={{0,1},{1,2},{2,3},{3,4},{4,5},{5,6},{6,7},{7,8},{8,9},{9,10},{10,1... | collective-permute-start | bytes 294920 | tf_op jit(solution)/shard_map/ppermute | solution.py:25
  4.1 1.7 %copy-start = (bf16[6144,192]{0,1:T(8,128)(2,1)S(1)}, bf16[6144,192]{0,1:T(8,128)(2,1)}, u32[]{:S(2)}) copy-start(bf16[6144,192]{0,1:T(8,128)(2,1)} %param.12) | copy-start | bytes 7077892
  5.8 1.2 %copy-start.2 = (bf16[4096,128]{1,0:T(8,128)(2,1)S(1)}, bf16[4096,128]{1,0:T(8,128)(2,1)}, u32[]{:S(2)}) copy-start(bf16[4096,128]{1,0:T(8,128)(2,1)} %vfirst_ref.3) | copy-start | bytes 3145732
  7.0 4.6 %copy-start.1 = (bf16[6144,192]{0,1:T(8,128)(2,1)S(1)}, bf16[6144,192]{0,1:T(8,128)(2,1)}, u32[]{:S(2)}) copy-start(bf16[6144,192]{0,1:T(8,128)(2,1)} %param.12) | copy-start | bytes 7077892
  7.0 4.6 %copy-start.3 = (bf16[4096,128]{1,0:T(8,128)(2,1)S(1)}, bf16[4096,128]{1,0:T(8,128)(2,1)}, u32[]{:S(2)}) copy-start(bf16[4096,128]{1,0:T(8,128)(2,1)} %vfirst_ref.3) | copy-start | bytes 3145732
  7.0 4.6 %copy-start.6 = (bf16[192,192]{1,0:T(8,128)(2,1)S(1)}, bf16[192,192]{1,0:T(8,128)(2,1)}, u32[]{:S(2)}) copy-start(bf16[192,192]{1,0:T(8,128)(2,1)} %ksecond_ref.1) | copy-start | bytes 221188
  7.0 4.6 %copy-start.7 = (bf16[128,128]{1,0:T(8,128)(2,1)S(1)}, bf16[128,128]{1,0:T(8,128)(2,1)}, u32[]{:S(2)}) copy-start(bf16[128,128]{1,0:T(8,128)(2,1)} %vsecond_ref.1) | copy-start | bytes 98308
  11.7 25.6 %copy-start.4 = (bf16[128,384]{1,0:T(8,128)(2,1)}, bf16[128,384]{1,0:T(8,128)(2,1)S(1)}, u32[]{:S(2)}) copy-start(bf16[128,384]{1,0:T(8,128)(2,1)S(1)} %collective-permute-done.before_ref.one_ref) | copy-start | bytes 294916
  32.6 4.4 %copy-start.10 = (s32[128,16]{0,1:T(8,128)S(1)}, s32[128,16]{0,1:T(8,128)}, u32[]{:S(2)}) copy-start(s32[128,16]{0,1:T(8,128)} %param.17) | copy-start | bytes 24580
  32.6 10.1 %copy-start.11 = (f32[16,2]{0,1:T(2,128)S(1)}, f32[16,2]{0,1:T(2,128)}, u32[]{:S(2)}) copy-start(f32[16,2]{0,1:T(2,128)} %param.16) | copy-start | bytes 388
  32.6 36.1 %all-to-all-start.1 = ((bf16[16,320,128]{2,1,0:T(8,128)(2,1)}), bf16[16,320,128]{2,1,0:T(8,128)(2,1)S(1)}, u32[]{:S(2)}, u32[]{:S(2)}) async-start(bf16[16,320,128]{2,1,0:T(8,128)(2,1)} %pack.1), calls=%async_computation.1 | async-start | bytes 2621440 | tf_op jit(solution)/shard_map/all_to_all | solution.py:500
  38.0 24.6 %collective-permute-start.2 = (bf16[256,384]{1,0:T(8,128)(2,1)}, bf16[256,384]{1,0:T(8,128)(2,1)}, u32[]{:S(2)}, u32[]{:S(2)}) collective-permute-start(bf16[256,384]{1,0:T(8,128)(2,1)} %pad_maximum_fusion), channel_id=1, source_target_pairs={{0,2},{1,3},{2,4},{3,5},{4,6},{5,7},{6,8},{7,9},{8,10},{9,11},{10,... | collective-permute-start | bytes 589832 | tf_op jit(solution)/shard_map/ppermute | solution.py:25
  45.1 12.5 %collective-permute-start.1 = (bf16[128,384]{1,0:T(8,128)(2,1)S(1)}, bf16[128,384]{1,0:T(8,128)(2,1)S(1)}, u32[]{:S(2)}, u32[]{:S(2)}) collective-permute-start(bf16[128,384]{1,0:T(8,128)(2,1)S(1)} %pair.1.pair_ref), channel_id=1, source_target_pairs={{0,4},{1,5},{2,6},{3,7},{4,8},{5,9},{6,10},{7,11},{8,12},{9,13},{1... | collective-permute-start | bytes 294920 | tf_op jit(solution)/shard_map/ppermute | solution.py:25
  62.6 0.9 %copy-start.5 = (bf16[128,384]{1,0:T(8,128)(2,1)S(1)}, bf16[128,384]{1,0:T(8,128)(2,1)}, u32[]{:S(2)}) copy-start(bf16[128,384]{1,0:T(8,128)(2,1)} %copy-done.4) | copy-start | bytes 294916
  67.8 1.0 %copy-start.8 = (f32[2048,128]{1,0:T(8,128)}, f32[2048,128]{1,0:T(8,128)S(1)}, u32[]{:S(2)}) copy-start(f32[2048,128]{1,0:T(8,128)S(1)} %window.1.win_ref) | copy-start | bytes 3145732
  68.8 7.8 %copy-start.9 = (f32[2048,128]{1,0:T(8,128)S(1)}, f32[2048,128]{1,0:T(8,128)}, u32[]{:S(2)}) copy-start(f32[2048,128]{1,0:T(8,128)} %copy-done.8) | copy-start | bytes 3145732
  68.8 7.8 %collective-permute-start.3 = (bf16[16,320,128]{2,1,0:T(8,128)(2,1)S(1)}, bf16[16,320,128]{2,1,0:T(8,128)(2,1)S(1)}, u32[]{:S(2)}, u32[]{:S(2)}) collective-permute-start(bf16[16,320,128]{2,1,0:T(8,128)(2,1)S(1)} %all-to-all-done.1.kv_ref), channel_id=1, source_target_pairs={{0,16},{16,0},{32,48},{48,32},{64,80},{80,64},{96,112},{112,96},{1... | collective-permute-start | bytes 3932168 | tf_op jit(solution)/shard_map/ppermute | solution.py:503
